TPU v7x, 32 devices: a whole 2x2x4 slice. The times are simulated.
32 devices in a mesh: pole: 4 (over x, core), grid: 8 (over z, y).
Axes of the slice: x: 2, y: 2, z: 4, core: 2. Of those that a mesh axis runs over, the one named last changes fastest.
Arguments:
- anc_inv: bfloat16 [4, 1536, 1536], P('pole', 'grid'), may hold values from -6 to 6
- factor_cols: bfloat16 [4, 8, 2, 256, 256], P('pole', 'grid'), may hold values from -0.25 to 0.25
- diag_inv: bfloat16 [4, 8, 256, 256], P('pole', 'grid'), may hold values from -6 to 6
- intersection: bfloat16 [8, 256, 256], P('grid'), may hold values from -0.0234375 to 0.0234375
- pole_w: float32 [4], P('pole'), may hold values from 0.5 to 2
- pole_z: float32 [4], P('pole'), may hold values from -2 to -0.5
- ancestors: int32 [8, 2], P('grid'), may hold values from 0 to 5, as said below
- counts: int32 [8], P('grid'), may hold values from 1 to 2
- hpattern: int32 [8, 2], P('grid'), may hold values 0 or 1
- siesta_of: int32 [2048], P('grid'), may hold values from 0 to 2047, as said below
- supernode_of: int32 [2048], P('grid'), may hold values from 0 to 2047, as said below
Outputs:
- density: bfloat16 [2048, 768], P('grid', 'pole')
- energy: bfloat16 [2048, 768], P('grid', 'pole')
- electrons: float32 [], replicated
Inputs may be any that keep to these rules, and one draw needn't show every extreme that they name: `ancestors`: the 2 entries of a row are distinct. `siesta_of`: A permutation; supernode K's 256 orbitals go to each block-column owner (index // 256) at most 32 times, and exactly 32 times to some owner. `supernode_of`: the inverse permutation of siesta_of.
All inputs are finite; a program needn't handle non-finite values. No bound on the sum of `hpattern` on one device may be relied on, other than what follows from the above.
Results may differ from a plain program's by a relative error of at most 0.001.
Values may be sent and summed in bfloat16 or wider, within the bound.
No kernel may reach another device: no remote copies, remote signals or barrier semaphores. Data moves between devices by JAX's collectives and lax.ppermute only.
A program may use at most 64 MiB of HBM per device.

v0:
```python
import jax
import jax.numpy as jnp
from jax import lax
from jax.sharding import PartitionSpec as P


def body(
    anc_inv,
    factor_cols,
    diag_inv,
    intersection,
    pole_w,
    pole_z,
    ancestors,
    counts,
    hpattern,
    siesta_of,
    supernode_of,
):
    width = diag_inv.shape[-1]
    anc_count = anc_inv.shape[2] // width
    blk_count = ancestors.shape[1]
    select = (ancestors[0][:, None] == jnp.arange(anc_count)[None, :]).astype(jnp.bfloat16)
    live_mask = (jnp.arange(blk_count) < counts[0]).astype(jnp.bfloat16)
    lower_cols = (factor_cols[0, 0] * live_mask[:, None, None]).reshape(blk_count * width, width)
    gathered = lax.all_gather(anc_inv[0], "grid", axis=0, tiled=True)
    row_count = gathered.shape[0]
    picked = jnp.einsum(
        "rnw,mn->rmw",
        gathered.reshape(row_count, anc_count, width),
        select,
        preferred_element_type=jnp.float32,
    ).astype(jnp.bfloat16)
    product = jnp.dot(
        picked.reshape(row_count, blk_count * width), lower_cols, preferred_element_type=jnp.float32
    )
    blocks = product.reshape(anc_count, width, width)
    chosen = -jnp.sum(select.astype(jnp.float32)[:, :, None, None] * blocks[None], axis=1)
    diag_block = diag_inv[0, 0].astype(jnp.float32) - jnp.dot(
        lower_cols.astype(jnp.float32).T,
        chosen.reshape(blk_count * width, width),
        precision=lax.Precision.HIGHEST,
        preferred_element_type=jnp.float32,
    )
    masked = chosen * hpattern[0].astype(jnp.float32)[:, None, None]
    stacked = jnp.concatenate([diag_block[None], masked], axis=0)
    cols_rows = stacked.transpose(2, 0, 1).reshape(width, (blk_count + 1) * width)
    own_count = pole_w[0] * jnp.sum(diag_block * intersection[0].astype(jnp.float32))
    electrons = lax.psum(own_count, ("pole", "grid"))
    dens_term = pole_w[0] * cols_rows
    energy_term = pole_z[0] * cols_rows
    dens_part, energy_part = (
        lax.psum_scatter(dens_term, "pole", scatter_dimension=1, tiled=True),
        lax.psum_scatter(energy_term, "pole", scatter_dimension=1, tiled=True),
    )
    row_width = dens_part.shape[1]
    grid_count = lax.axis_size("grid")
    slot_cap = (width + grid_count - 1) // grid_count
    positions = jnp.arange(width)
    dest_owner = siesta_of // width
    same_dest = dest_owner[:, None] == dest_owner[None, :]
    earlier = positions[:, None] > positions[None, :]
    send_rank = jnp.sum((same_dest & earlier).astype(jnp.int32), axis=1)
    send_slot = dest_owner * slot_cap + send_rank
    placement = (jnp.arange(grid_count * slot_cap)[:, None] == send_slot[None, :]).astype(
        jnp.bfloat16
    )
    send_dens = (
        jnp.dot(placement, dens_part.astype(jnp.bfloat16), preferred_element_type=jnp.float32)
        .astype(jnp.bfloat16)
        .reshape(grid_count, slot_cap, row_width)
    )
    send_energy = (
        jnp.dot(placement, energy_part.astype(jnp.bfloat16), preferred_element_type=jnp.float32)
        .astype(jnp.bfloat16)
        .reshape(grid_count, slot_cap, row_width)
    )
    recv_dens, recv_energy = (
        lax.all_to_all(send_dens, "grid", split_axis=0, concat_axis=0, tiled=True),
        lax.all_to_all(send_energy, "grid", split_axis=0, concat_axis=0, tiled=True),
    )
    source_dev = supernode_of // width
    same_source = source_dev[:, None] == source_dev[None, :]
    before = supernode_of[None, :] < supernode_of[:, None]
    recv_rank = jnp.sum((same_source & before).astype(jnp.int32), axis=1)
    recv_slot = source_dev * slot_cap + recv_rank
    pickup = (recv_slot[:, None] == jnp.arange(grid_count * slot_cap)[None, :]).astype(jnp.bfloat16)
    density = jnp.dot(
        pickup,
        recv_dens.reshape(grid_count * slot_cap, row_width),
        preferred_element_type=jnp.float32,
    ).astype(jnp.bfloat16)
    energy = jnp.dot(
        pickup,
        recv_energy.reshape(grid_count * slot_cap, row_width),
        preferred_element_type=jnp.float32,
    ).astype(jnp.bfloat16)
    return (density, energy, electrons)


def solution(mesh):
    placed = (
        P("pole", "grid", None),
        P("pole", "grid", None, None, None),
        P("pole", "grid", None, None),
        P("grid", None, None),
        P("pole"),
        P("pole"),
        P("grid", None),
        P("grid"),
        P("grid", None),
        P("grid"),
        P("grid"),
    )
    return jax.shard_map(
        body,
        mesh=mesh,
        in_specs=placed,
        out_specs=(P("grid", "pole"), P("grid", "pole"), P()),
        check_vma=False,
    )
```

profile of v0, /device:TPU:0, one launch (start us, length us, event | category | flops | bytes accessed | tf_op | source)
XLA Modules:
  0.0 190.2 jit_solution(11743723445649057235)
XLA Ops:
  7.2 0.0 all-gather.3.cloned.1.call-start
  7.2 0.7 all-gather.3.cloned.1.call-update
  7.9 0.0 reduce-scatter.5.cloned.1.call-start
  9.9 0.7 convert_bitcast_fusion
  10.6 0.7 fusion.16
  11.3 1.0 broadcast_multiply_fusion
  12.3 79.9 %all-gather.3.cloned.1.call-done = bf16[1,1536,1536]{2,1,0:T(8,128)(2,1)} async-done(((bf16[1,192,1536]{2,1,0:T(8,128)(2,1)}), bf16[1,1536,1536]{2,1,0:T(8,128)(2,1)}) %all-gather.3.cloned.1.call-update) | async-done | bytes 4718608 | tf_op jit(solution)/shard_map/all_gather | solution.py:26
  92.2 6.7 %copy.25 = bf16[1,1536,1536]{1,2,0:T(8,128)(2,1)} copy(bf16[1,1536,1536]{2,1,0:T(8,128)(2,1)} %all-gather.3.cloned.1.call-done) | data formatting | bytes 9437184 | tf_op jit(solution)/shard_map/all_gather | solution.py:26
  99.0 0.0 copy-start.5
  99.0 8.7 %copy.26 = bf16[1536,6,256]{2,1,0:T(8,128)(2,1)} copy(bf16[1536,6,256]{0,2,1:T(8,128)(2,1)} %bitcast.50) | data formatting | bytes 9437184 | tf_op jit(solution)/shard_map/reshape | solution.py:30
  107.6 0.0 copy-done.5
  107.6 4.6 %fusion = bf16[1536,2,256]{2,1,0:T(2,128)(2,1)S(1)} fusion(bf16[1536,6,256]{2,1,0:T(8,128)(2,1)} %copy.26, s32[2]{0:T(128)S(1)} %bitcast.58), kind=kOutput, calls=%fused_computation.2 | convolution fusion | flops 10223628 | bytes 6291464 | tf_op jit(solution)/shard_map/rnw,mn->rmw/dot_general | solution.py:28
  112.3 1.1 reshape.95
  113.3 0.0 copy-start
  113.3 0.0 copy-start.1
  113.3 0.0 copy-start.2
  113.4 0.6 fusion.18
  113.9 0.3 multiply_reduce_fusion
  114.2 0.0 copy-start.4
  114.2 0.0 copy-start.3
  114.2 0.1 negate_multiply_fusion
  114.4 0.0 copy-done
  114.4 0.0 copy-done.1
  114.4 0.0 copy-done.2
  114.4 1.2 fusion.5
  115.5 1.3 fusion.2
  116.9 0.0 reduce-scatter.5.cloned.1.call-update
  116.9 0.0 reduce-scatter.3.cloned.1.call-start
  116.9 0.7 reduce-scatter.3.cloned.1.call-update
  117.6 0.0 copy-done.4
  117.6 0.2 convert_reduce_fusion
  117.8 0.0 copy-done.3
  117.8 0.2 convert_reduce_fusion.1
  118.7 38.6 %psum.7 = f32[]{:T(128)} all-reduce(f32[]{:T(128)S(6)} %mul.94), channel_id=1, replica_groups=mesh['pole'=4,'grid'=8] {'pole','grid'}, use_global_device_ids=true, to_apply=%region_6.7 | all-reduce | flops 1 | bytes 8 | tf_op jit(solution)/shard_map/psum | solution.py:49
  157.4 0.0 reduce-scatter.5.cloned.1.call-done
  157.4 1.1 convolution_convert_fusion.2
  158.5 0.8 copy.29
  159.3 5.5 %all-to-all-start.1 = ((bf16[8,32,192]{2,1,0:T(8,128)(2,1)}), bf16[8,32,192]{2,1,0:T(8,128)(2,1)S(1)}, u32[]{:S(2)}, u32[]{:S(2)}) async-start(bf16[8,32,192]{2,1,0:T(8,128)(2,1)} %bitcast.20), calls=%async_computation.3 | async-start | bytes 262144 | tf_op jit(solution)/shard_map/all_to_all | solution.py:80
  164.8 0.0 reduce-scatter.3.cloned.1.call-done
  164.8 1.1 convolution_convert_fusion.4
  165.9 0.8 copy.28
  166.7 5.4 %all-to-all-done.1 = bf16[8,32,192]{2,1,0:T(8,128)(2,1)S(1)} async-done(((bf16[8,32,192]{2,1,0:T(8,128)(2,1)}), bf16[8,32,192]{2,1,0:T(8,128)(2,1)S(1)}, u32[]{:S(2)}, u32[]{:S(2)}) %all-to-all-start.1) | async-done | bytes 98336 | tf_op jit(solution)/shard_map/all_to_all | solution.py:80
  172.1 3.4 %all-to-all-start = ((bf16[8,32,192]{2,1,0:T(8,128)(2,1)}), bf16[8,32,192]{2,1,0:T(8,128)(2,1)S(1)}, u32[]{:S(2)}, u32[]{:S(2)}) async-start(bf16[8,32,192]{2,1,0:T(8,128)(2,1)} %bitcast.15), calls=%async_computation.1 | async-start | bytes 262144 | tf_op jit(solution)/shard_map/all_to_all | solution.py:79
  175.5 0.9 convolution_convert_fusion.1
  176.4 6.3 %all-to-all-done = bf16[8,32,192]{2,1,0:T(8,128)(2,1)S(1)} async-done(((bf16[8,32,192]{2,1,0:T(8,128)(2,1)}), bf16[8,32,192]{2,1,0:T(8,128)(2,1)S(1)}, u32[]{:S(2)}, u32[]{:S(2)}) %all-to-all-start) | async-done | bytes 98336 | tf_op jit(solution)/shard_map/all_to_all | solution.py:79
  182.8 0.9 convolution_convert_fusion.3
  (5 shorter events, 0.0 us)
Async XLA Ops:
  7.2 85.1 %all-gather.3.cloned.1.call-start = ((), (), s32[]{:S(2)}) async-start(), calls=%async_computation.6 | async-start | bytes 5308416 | tf_op jit(solution)/shard_map/all_gather | solution.py:26
  7.9 149.5 %reduce-scatter.5.cloned.1.call-start = ((), (), s32[]{:S(2)}) async-start(), calls=%async_computation.5 | async-start | bytes 983040 | tf_op jit(solution)/shard_map/reduce_scatter | solution.py:54
  99.0 8.7 %copy-start.5 = (s32[1,2]{1,0:T(1,128)S(1)}, s32[1,2]{1,0:T(1,128)}, u32[]{:S(2)}) copy-start(s32[1,2]{1,0:T(1,128)} %param.17) | copy-start | bytes 28
  113.3 1.0 copy-start
  113.3 1.0 copy-start.1
  113.3 1.0 copy-start.2
  114.2 3.4 %copy-start.4 = (s32[256]{0:T(256)S(1)}, s32[256]{0:T(256)}, u32[]{:S(2)}) copy-start(s32[256]{0:T(256)} %param.20) | copy-start | bytes 3076
  114.2 3.6 %copy-start.3 = (s32[256]{0:T(256)S(1)}, s32[256]{0:T(256)}, u32[]{:S(2)}) copy-start(s32[256]{0:T(256)} %param.21) | copy-start | bytes 3076
  116.9 47.9 %reduce-scatter.3.cloned.1.call-start = ((), (), s32[]{:S(2)}) async-start(), calls=%async_computation.4 | async-start | bytes 983040 | tf_op jit(solution)/shard_map/reduce_scatter | solution.py:53
  159.3 12.8 %all-to-all-start.1 = ((bf16[8,32,192]{2,1,0:T(8,128)(2,1)}), bf16[8,32,192]{2,1,0:T(8,128)(2,1)S(1)}, u32[]{:S(2)}, u32[]{:S(2)}) async-start(bf16[8,32,192]{2,1,0:T(8,128)(2,1)} %bitcast.20), calls=%async_computation.3 | async-start | bytes 262144 | tf_op jit(solution)/shard_map/all_to_all | solution.py:80
  172.1 10.7 %all-to-all-start = ((bf16[8,32,192]{2,1,0:T(8,128)(2,1)}), bf16[8,32,192]{2,1,0:T(8,128)(2,1)S(1)}, u32[]{:S(2)}, u32[]{:S(2)}) async-start(bf16[8,32,192]{2,1,0:T(8,128)(2,1)} %bitcast.15), calls=%async_computation.1 | async-start | bytes 262144 | tf_op jit(solution)/shard_map/all_to_all | solution.py:79
Sparse Core Ops, SparseCore 0:
  10.2 82.0 all-gather.2
  117.0 21.6 reduce-scatter.4
  141.2 23.1 reduce-scatter.2
where the time goes:
time: 191 us; the launch traced here: 190 us
  waiting for transfers between devices  93.1 us (49%)
  blocking collectives  38.6 us (20%)
  local copies, waits for them, and re-layouts  18 us (9%)
  between operations  16.5 us (9%)
  matrix products  10.5 us (5%)
  starting transfers between devices  8.97 us (5%)
  other arithmetic  4.55 us (2%)
    all_gather x1, waiting for transfers between devices, body(): gathered = lax.all_gather(anc_inv[0], 'grid', axis=0, tiled=True)  79.9 us
    psum x1, blocking collectives, body(): electrons = lax.psum(own_count, ('pole', 'grid'))  38.6 us
    reshape x1, local copies, waits for them, and re-layouts, body(): gathered.reshape(row_count, anc_count, width)  8.66 us
    all_gather x1, local copies, waits for them, and re-layouts, body(): gathered = lax.all_gather(anc_inv[0], 'grid', axis=0, tiled=True)  6.72 us
    all_to_all x1, waiting for transfers between devices, body(): lax.all_to_all(send_dens, 'grid', split_axis=0, concat_axis=0, tiled=True)  6.35 us
    all_to_all x1, starting transfers between devices, body(): lax.all_to_all(send_energy, 'grid', split_axis=0, concat_axis=0, tiled=True)  5.48 us
    all_to_all x1, waiting for transfers between devices, body(): lax.all_to_all(send_energy, 'grid', split_axis=0, concat_axis=0, tiled=True)  5.42 us
    dot_general x1, matrix products, body(): jnp.einsum('rnw,mn->rmw', gathered.reshape(row_count, anc_count, width),...  4.62 us
  transfers between devices with their start and end apart: 5, of which 3 were waited for; matrix products, arithmetic and copies ran while one was open for 4% of the time, Pallas kernels for 0%

commit v1 on v0

v1 whole, which is shorter than its diff:
```python
import functools

import jax
import jax.numpy as jnp
from jax import lax
from jax.experimental import pallas as pl
from jax.experimental.pallas import tpu as pltpu
from jax.sharding import PartitionSpec as P

VMEM = pltpu.VMEM
SMEM = pltpu.SMEM
LANES = 128
SUB = 8


def vspec():
    return pl.BlockSpec(memory_space=VMEM)


def sspec():
    return pl.BlockSpec(memory_space=SMEM)


def select_kernel(width, rows, blk_count, table_ref, spread_ref, out_ref):
    for dest in range(out_ref.shape[0]):
        for row_blk in range(blk_count):
            row_at = pl.multiple_of(table_ref[dest, row_blk] * rows, rows)
            for col_blk in range(blk_count):
                col_at = pl.multiple_of(table_ref[dest, col_blk] * width, width)
                out_ref[
                    dest,
                    row_blk * rows : (row_blk + 1) * rows,
                    col_blk * width : (col_blk + 1) * width,
                ] = spread_ref[pl.ds(row_at, rows), pl.ds(col_at, width)]


def columns_kernel(
    shares,
    chunk,
    counts_ref,
    hpattern_ref,
    weight_ref,
    energy_ref,
    rows_ref,
    factor_ref,
    diag_ref,
    inter_ref,
    out_ref,
    off_ref,
):
    blk_count, width, _ = factor_ref.shape
    parts = [
        factor_ref[m] * (m < counts_ref[0]).astype(jnp.float32).astype(jnp.bfloat16)
        for m in range(blk_count)
    ]
    lower = jnp.concatenate(parts, axis=0)
    product = jnp.dot(rows_ref[...], lower, preferred_element_type=jnp.float32)
    per_blk = width // shares
    for m in range(blk_count):
        scale = hpattern_ref[0, m].astype(jnp.float32)
        for j in range(shares):
            for c in range(per_blk // SUB):
                at = (j * blk_count + m) * per_blk + c * SUB
                piece = -product[at : at + SUB]
                row = m * width + (c * shares + j) * SUB
                off_ref[row : row + SUB, :] = piece
                place = width + row
                out_ref[place // chunk, place % chunk : place % chunk + SUB, :] = piece * scale
    off = off_ref[...]
    high = off.astype(jnp.bfloat16)
    rest = off - high.astype(jnp.float32)
    mid = rest.astype(jnp.bfloat16)
    low = (rest - mid.astype(jnp.float32)).astype(jnp.bfloat16)
    contract = functools.partial(
        lax.dot_general,
        dimension_numbers=(((0,), (0,)), ((), ())),
        preferred_element_type=jnp.float32,
    )
    product_sum = contract(lower, low) + contract(lower, mid) + contract(lower, high)
    diag_block = diag_ref[...].astype(jnp.float32) - product_sum
    at = 0
    while at < width:
        size = min(chunk - at % chunk, width - at)
        out_ref[at // chunk, at % chunk : at % chunk + size, :] = diag_block[at : at + size]
        at += size
    count = weight_ref[0] * jnp.sum(diag_block * inter_ref[...].astype(jnp.float32))
    row_id = lax.broadcasted_iota(jnp.int32, (SUB, width), 0)
    extra = jnp.where(row_id == 0, weight_ref[0], jnp.where(row_id == 1, energy_ref[0], count))
    for q in range(out_ref.shape[0]):
        out_ref[q, chunk : chunk + SUB, :] = extra


def place_kernel(slot_cap, dests, slot_ref, stack_ref, out_ref):
    poles, rows, width = stack_ref.shape
    chunk = rows - SUB
    dens = jnp.zeros((chunk, width), jnp.float32)
    energy = jnp.zeros((chunk, width), jnp.float32)
    count = jnp.zeros((1, width), jnp.float32)
    for p in range(poles):
        term = stack_ref[p, :chunk, :]
        dens = dens + stack_ref[p, chunk : chunk + 1, :] * term
        energy = energy + stack_ref[p, chunk + 1 : chunk + 2, :] * term
        count = count + stack_ref[p, chunk + 2 : chunk + 3, :]
    both = jnp.concatenate([dens, energy], axis=0).astype(jnp.bfloat16)
    total, lanes = out_ref.shape
    slots = total // dests
    one_hot = (lax.broadcasted_iota(jnp.int32, (total, width), 0) == slot_ref[...]).astype(
        jnp.bfloat16
    )
    placed = lax.dot_general(
        one_hot, both, (((1,), (1,)), ((), ())), preferred_element_type=jnp.float32
    )
    own = count[:, 0:1]
    high = own.astype(jnp.bfloat16).astype(jnp.float32)
    rest = own - high
    mid = rest.astype(jnp.bfloat16).astype(jnp.float32)
    lane = lax.broadcasted_iota(jnp.int32, (1, lanes), 1)
    pieces = jnp.where(lane == 0, high, jnp.where(lane == 1, mid, rest - mid))
    pieces = jnp.where(lane < 3, pieces, 0.0)
    row = lax.broadcasted_iota(jnp.int32, (total, 1), 0)
    marked = functools.reduce(
        jnp.logical_or, [row == g * slots + slot_cap for g in range(dests)]
    )
    out_ref[...] = jnp.where(marked, pieces, placed).astype(jnp.bfloat16)


def pickup_kernel(slot_cap, dests, slot_ref, recv_ref, dens_ref, energy_ref, count_ref):
    total, lanes = recv_ref.shape
    slots = total // dests
    chunk = lanes // 2
    width = slot_ref.shape[1]
    recv = recv_ref[...]
    one_hot = (lax.broadcasted_iota(jnp.int32, (total, width), 0) == slot_ref[...]).astype(
        jnp.bfloat16
    )
    out = lax.dot_general(
        recv, one_hot, (((0,), (0,)), ((), ())), preferred_element_type=jnp.float32
    ).astype(jnp.bfloat16)
    dens_ref[...] = out[:chunk]
    energy_ref[...] = out[chunk:]
    row = lax.broadcasted_iota(jnp.int32, (total, 1), 0)
    marked = functools.reduce(
        jnp.logical_or, [row == g * slots + slot_cap for g in range(dests)]
    )
    pieces = jnp.where(marked, recv[:, :LANES].astype(jnp.float32), 0.0)
    count_ref[0, 0] = jnp.sum(pieces)


def ranks(own, order):
    same = own[:, None] == own[None, :]
    earlier = order[None, :] < order[:, None]
    return jnp.sum((same & earlier).astype(jnp.int32), axis=1)


def body(
    anc_inv,
    factor_cols,
    diag_inv,
    intersection,
    pole_w,
    pole_z,
    ancestors,
    counts,
    hpattern,
    siesta_of,
    supernode_of,
):
    width = diag_inv.shape[-1]
    local_rows, anc_rows = anc_inv.shape[1:]
    blk_count = ancestors.shape[1]
    grid_count = lax.axis_size("grid")
    pole_count = lax.axis_size("pole")
    chunk = (blk_count + 1) * width // pole_count
    slot_cap = (width + grid_count - 1) // grid_count
    slots = slot_cap + (SUB if slot_cap % SUB == 0 else 1)

    dest_owner = siesta_of // width
    send_slot = dest_owner * slots + ranks(dest_owner, jnp.arange(width))
    source_dev = supernode_of // width
    recv_slot = source_dev * slots + ranks(source_dev, supernode_of)

    spread = grid_count * SUB
    if local_rows % spread == 0 and width % spread == 0:
        shares = grid_count
        mine = anc_inv[0].reshape(local_rows // spread, grid_count, SUB, anc_rows)
        mine = mine.transpose(1, 0, 2, 3).reshape(grid_count, local_rows // grid_count, anc_rows)
        table = jnp.broadcast_to(
            jnp.pad(ancestors, ((0, 0), (0, LANES - blk_count))).astype(jnp.bfloat16)[None],
            (grid_count, local_rows // grid_count, LANES),
        )
        sent = jnp.concatenate([mine, table], axis=2)
        held = lax.all_to_all(sent, "grid", split_axis=0, concat_axis=0, tiled=True)
        all_anc = held[:, 0, anc_rows : anc_rows + blk_count].astype(jnp.int32)
        rows = width // grid_count
        chosen = pl.pallas_call(
            functools.partial(select_kernel, width, rows, blk_count),
            out_shape=jax.ShapeDtypeStruct(
                (grid_count, blk_count * rows, blk_count * width), jnp.bfloat16
            ),
            in_specs=[sspec(), vspec()],
            out_specs=vspec(),
            name="select",
        )(all_anc, held.reshape(local_rows, anc_rows + LANES))
        sub_block = lax.all_to_all(chosen, "grid", split_axis=0, concat_axis=0, tiled=True)
    else:
        shares = 1
        gathered = lax.all_gather(anc_inv[0], "grid", axis=0, tiled=True)
        blocks = gathered.reshape(anc_rows // width, width, anc_rows // width, width)
        sub_block = jnp.take(jnp.take(blocks, ancestors[0], axis=0), ancestors[0], axis=2)
    sub_block = sub_block.reshape(blk_count * width, blk_count * width)

    stack = pl.pallas_call(
        functools.partial(columns_kernel, shares, chunk),
        out_shape=jax.ShapeDtypeStruct((pole_count, chunk + SUB, width), jnp.float32),
        in_specs=[sspec()] * 4 + [vspec()] * 4,
        out_specs=vspec(),
        scratch_shapes=[VMEM((blk_count * width, width), jnp.float32)],
        name="columns",
    )(
        counts,
        hpattern,
        pole_w,
        pole_z,
        sub_block,
        factor_cols[0, 0],
        diag_inv[0, 0],
        intersection[0],
    )
    stack = lax.all_to_all(stack, "pole", split_axis=0, concat_axis=0, tiled=True)

    total = grid_count * slots
    placed = pl.pallas_call(
        functools.partial(place_kernel, slot_cap, grid_count),
        out_shape=jax.ShapeDtypeStruct((total, 2 * chunk), jnp.bfloat16),
        in_specs=[vspec(), vspec()],
        out_specs=vspec(),
        name="place",
    )(send_slot[None], stack)
    arrived = lax.all_to_all(
        placed.reshape(grid_count, slots, 2 * chunk),
        "grid",
        split_axis=0,
        concat_axis=0,
        tiled=True,
    )
    density, energy, electrons = pl.pallas_call(
        functools.partial(pickup_kernel, slot_cap, grid_count),
        out_shape=(
            jax.ShapeDtypeStruct((chunk, width), jnp.bfloat16),
            jax.ShapeDtypeStruct((chunk, width), jnp.bfloat16),
            jax.ShapeDtypeStruct((1, 1), jnp.float32),
        ),
        in_specs=[vspec(), vspec()],
        out_specs=(vspec(), vspec(), sspec()),
        name="pickup",
    )(recv_slot[None], arrived.reshape(total, 2 * chunk))
    return (density.T, energy.T, electrons[0, 0])


def solution(mesh):
    placed = (
        P("pole", "grid", None),
        P("pole", "grid", None, None, None),
        P("pole", "grid", None, None),
        P("grid", None, None),
        P("pole"),
        P("pole"),
        P("grid", None),
        P("grid"),
        P("grid", None),
        P("grid"),
        P("grid"),
    )
    return jax.shard_map(
        body,
        mesh=mesh,
        in_specs=placed,
        out_specs=(P("grid", "pole"), P("grid", "pole"), P()),
        check_vma=False,
    )
```

time: 191 us -> 84.5 us (0.44)
  waiting for transfers between devices: 93.1 us -> 30.8 us
  blocking collectives: 38.6 us -> 24.5 us
  between operations: 16.5 us -> 2.68 us
  local copies, waits for them, and re-layouts: 18 us -> 4.34 us
  matrix products: 10.5 us -> 0 us
  Pallas kernels: 0 us -> 9.16 us
  other arithmetic: 4.55 us -> 1.7 us
    all_gather x1 -> x0, waiting for transfers between devices: 79.9 us -> none  [body(): gathered = lax.all_gather(anc_inv[0], 'grid', axis=0, tiled=True)]
    psum x1 -> x0, blocking collectives: 38.6 us -> none  [body(): electrons = lax.psum(own_count, ('pole', 'grid'))]
    all_to_all x0 -> x1, blocking collectives: none -> 24.5 us  [body(): held = lax.all_to_all(sent, 'grid', split_axis=0, concat_axis=0, tiled=True)]
    all_to_all x2 -> x3, waiting for transfers between devices: 11.8 us -> 30.8 us  [the longest x1 12.1 us: body(): lax.all_to_all(chosen, 'grid', split_axis=0, concat_axis=0, tiled=True)]
    dot_general x7 -> x0, matrix products: 10.5 us -> none  [the longest x1 4.62 us: body(): jnp.einsum('rnw,mn->rmw', gathered.reshape(row_count, anc_count, width),...]
    pallas_call x0 -> x4, Pallas kernels: none -> 9.16 us  [the longest x1 3.13 us: body(): pl.pallas_call(functools.partial(columns_kernel, shares, chunk), out_shap...]
    reshape x1 -> x0, local copies, waits for them, and re-layouts: 8.66 us -> none  [body(): gathered.reshape(row_count, anc_count, width)]
    all_gather x1 -> x0, local copies, waits for them, and re-layouts: 6.72 us -> none  [body(): gathered = lax.all_gather(anc_inv[0], 'grid', axis=0, tiled=True)]
  transfers between devices with their start and end apart: 5 -> 3, of which waited for: 3 -> 3; matrix products, arithmetic and copies ran while one was open for 4% -> 2% of each run, Pallas kernels for 0% -> 0%
where the time goes in v1:
time: 84.5 us; the launch traced here: 84 us
  waiting for transfers between devices  30.8 us (36%)
  blocking collectives  24.5 us (29%)
  starting transfers between devices  10.8 us (13%)
  Pallas kernels  9.16 us (11%)
  local copies, waits for them, and re-layouts  4.34 us (5%)
  between operations  2.68 us (3%)
  other arithmetic  1.7 us (2%)
    all_to_all x1, blocking collectives, body(): held = lax.all_to_all(sent, 'grid', split_axis=0, concat_axis=0, tiled=True)  24.5 us
    all_to_all x1, waiting for transfers between devices, body(): lax.all_to_all(chosen, 'grid', split_axis=0, concat_axis=0, tiled=True)  12.1 us
    all_to_all x1, waiting for transfers between devices, body(): lax.all_to_all(stack, 'pole', split_axis=0, concat_axis=0, tiled=True)  11.1 us
    all_to_all x1, waiting for transfers between devices, body(): lax.all_to_all(placed.reshape(grid_count, slots, 2 * chunk), 'grid', spli...  7.56 us
    all_to_all x1, starting transfers between devices, body(): lax.all_to_all(placed.reshape(grid_count, slots, 2 * chunk), 'grid', spli...  3.63 us
    all_to_all x1, starting transfers between devices, body(): lax.all_to_all(stack, 'pole', split_axis=0, concat_axis=0, tiled=True)  3.63 us
    all_to_all x1, starting transfers between devices, body(): lax.all_to_all(chosen, 'grid', split_axis=0, concat_axis=0, tiled=True)  3.49 us
    pallas_call x1, Pallas kernels, body(): pl.pallas_call(functools.partial(columns_kernel, shares, chunk), out_shap...  3.13 us
  transfers between devices with their start and end apart: 3, of which 3 were waited for; matrix products, arithmetic and copies ran while one was open for 2% of the time, Pallas kernels for 0%

profile of v1, /device:TPU:0, one launch (start us, length us, event | category | flops | bytes accessed | tf_op | source)
XLA Modules:
  0.0 84.0 jit_solution(6683669838307133175)
XLA Ops:
  0.6 0.0 copy-start.6
  0.6 1.1 %copy.28 = bf16[3,8,8,1536]{3,2,0,1:T(8,128)(2,1)S(1)} copy(bf16[3,8,8,1536]{3,2,1,0:T(8,128)(2,1)} %bitcast.28) | data formatting | bytes 1179648 | tf_op jit(solution)/shard_map/reshape;squeeze | solution.py:185
  1.8 0.0 copy-done.6
  1.8 0.1 pad_maximum_fusion
  1.9 24.5 %all_to_all.20 = bf16[8,24,1664]{2,1,0:T(8,128)(2,1)S(1)} all-to-all(bf16[8,24,1664]{2,1,0:T(8,128)(2,1)S(1)} %pad_maximum_fusion), channel_id=1, replica_groups=mesh['pole'=4,'grid'=8] {'grid'}, dimensions={0} | all-to-all | bytes 1277952 | tf_op jit(solution)/shard_map/all_to_all | solution.py:192
  26.4 0.0 copy-start.1
  26.4 0.1 copy.26
  26.5 0.7 copy.25.table_ref
  27.2 0.0 copy-done.1
  27.2 1.9 %select.10 = bf16[8,64,512]{2,1,0:T(8,128)(2,1)} custom-call(s32[8,2]{1,0:T(8,128)} %copy.25.table_ref, bf16[192,1664]{1,0:T(8,128)(2,1)} %bitcast.23), custom_call_target="tpu_custom_call" | custom-call | tf_op jit(solution)/shard_map/select/pallas_call | solution.py:195
  29.2 3.5 %all-to-all-start.1 = ((bf16[8,64,512]{2,1,0:T(8,128)(2,1)}), bf16[8,64,512]{2,1,0:T(8,128)(2,1)S(1)}, u32[]{:S(2)}, u32[]{:S(2)}) async-start(bf16[8,64,512]{2,1,0:T(8,128)(2,1)} %select.10), calls=%async_computation.1 | async-start | bytes 1048576 | tf_op jit(solution)/shard_map/all_to_all | solution.py:204
  34.6 12.1 %all-to-all-done.1 = bf16[8,64,512]{2,1,0:T(8,128)(2,1)S(1)} async-done(((bf16[8,64,512]{2,1,0:T(8,128)(2,1)}), bf16[8,64,512]{2,1,0:T(8,128)(2,1)S(1)}, u32[]{:S(2)}, u32[]{:S(2)}) %all-to-all-start.1) | async-done | bytes 524320 | tf_op jit(solution)/shard_map/all_to_all | solution.py:204
  46.8 0.0 copy-start.2
  46.8 0.8 copy-done.2
  47.6 3.1 %columns.1 = f32[4,200,256]{2,1,0:T(8,128)} custom-call(s32[1]{0:T(128)S(6)} %copy.31.counts_ref, s32[1,2]{1,0:T(1,128)} %hpattern_ref.1, f32[1]{0:T(128)S(6)} %copy.29.weight_ref, f32[1]{0:T(128)S(6)} %copy.30.energy_ref, bf16[512,512]{1,0:T(8,128)(2,1)} %bitcast.25, bf16[2,256,256]{2,1,0:T(8,128)(2,1)} %bitcast.29, bf16[256,256]{1,0:T(8,128)(2,1)} %bitcast.30, ...), custom_call_target="tpu_custom_call" | custom-call | tf_op jit(solution)/shard_map/columns/pallas_call | solution.py:212
  50.7 0.0 copy-start.5
  50.7 3.6 %all-to-all-start.2 = ((f32[4,200,256]{2,1,0:T(8,128)}), f32[4,200,256]{2,1,0:T(8,128)S(1)}, u32[]{:S(2)}, u32[]{:S(2)}) async-start(f32[4,200,256]{2,1,0:T(8,128)} %columns.1), calls=%async_computation.2 | async-start | bytes 1638400 | tf_op jit(solution)/shard_map/all_to_all | solution.py:229
  54.3 0.0 copy-done.5
  54.3 0.0 copy-start.4
  54.4 0.2 convert_reduce_fusion
  54.5 0.6 multiply_add_fusion
  55.1 11.1 %all-to-all-done.2.stack_ref = f32[4,200,256]{2,1,0:T(8,128)S(1)} async-done(((f32[4,200,256]{2,1,0:T(8,128)}), f32[4,200,256]{2,1,0:T(8,128)S(1)}, u32[]{:S(2)}, u32[]{:S(2)}) %all-to-all-start.2) | async-done | bytes 819232 | tf_op jit(solution)/shard_map/all_to_all | solution.py:229
  66.3 0.0 copy-start
  66.3 0.9 %copy-done = f32[4,200,256]{2,1,0:T(8,128)} copy-done((f32[4,200,256]{2,1,0:T(8,128)}, f32[4,200,256]{2,1,0:T(8,128)S(1)}, u32[]{:S(2)}) %copy-start) | copy-done | bytes 819224
  67.2 2.2 %place.1 = bf16[320,384]{1,0:T(8,128)(2,1)} custom-call(s32[1,256]{1,0:T(1,128)} %bitcast.33, f32[4,200,256]{2,1,0:T(8,128)} %copy-done), custom_call_target="tpu_custom_call" | custom-call | tf_op jit(solution)/shard_map/place/pallas_call | solution.py:232
  69.3 3.6 %all-to-all-start.3 = ((bf16[8,40,384]{2,1,0:T(8,128)(2,1)}), bf16[8,40,384]{2,1,0:T(8,128)(2,1)S(1)}, u32[]{:S(2)}, u32[]{:S(2)}) async-start(bf16[8,40,384]{2,1,0:T(8,128)(2,1)} %bitcast.27), calls=%async_computation.3 | async-start | bytes 491520 | tf_op jit(solution)/shard_map/all_to_all | solution.py:239
  73.0 0.0 copy-done.4
  73.0 0.2 convert_reduce_fusion.1
  73.2 0.6 multiply_add_fusion.1
  73.8 7.6 %all-to-all-done.3 = bf16[8,40,384]{2,1,0:T(8,128)(2,1)S(1)} async-done(((bf16[8,40,384]{2,1,0:T(8,128)(2,1)}), bf16[8,40,384]{2,1,0:T(8,128)(2,1)S(1)}, u32[]{:S(2)}, u32[]{:S(2)}) %all-to-all-start.3) | async-done | bytes 245792 | tf_op jit(solution)/shard_map/all_to_all | solution.py:239
  81.4 0.0 copy-start.3
  81.4 0.7 copy-done.3
  82.0 1.9 %pickup.1 = (bf16[192,256]{1,0:T(8,128)(2,1)}, bf16[192,256]{1,0:T(8,128)(2,1)}, f32[1,1]{1,0:T(1,128)}) custom-call(s32[1,256]{1,0:T(1,128)} %bitcast.32, bf16[320,384]{1,0:T(8,128)(2,1)} %bitcast.26), custom_call_target="tpu_custom_call" | custom-call | tf_op jit(solution)/shard_map/pickup/pallas_call | solution.py:246
  (7 shorter events, 0.1 us)
Async XLA Ops:
  0.6 1.1 %copy-start.6 = (s32[1,2]{1,0:T(1,128)S(1)}, s32[1,2]{1,0:T(1,128)}, u32[]{:S(2)}) copy-start(s32[1,2]{1,0:T(1,128)} %param.17) | copy-start | bytes 28
  26.4 0.8 copy-start.1
  29.2 17.6 %all-to-all-start.1 = ((bf16[8,64,512]{2,1,0:T(8,128)(2,1)}), bf16[8,64,512]{2,1,0:T(8,128)(2,1)S(1)}, u32[]{:S(2)}, u32[]{:S(2)}) async-start(bf16[8,64,512]{2,1,0:T(8,128)(2,1)} %select.10), calls=%async_computation.1 | async-start | bytes 1048576 | tf_op jit(solution)/shard_map/all_to_all | solution.py:204
  46.8 0.8 copy-start.2
  50.7 3.6 %copy-start.5 = (s32[256]{0:T(256)S(1)}, s32[256]{0:T(256)}, u32[]{:S(2)}) copy-start(s32[256]{0:T(256)} %param.20) | copy-start | bytes 3076
  50.7 15.6 %all-to-all-start.2 = ((f32[4,200,256]{2,1,0:T(8,128)}), f32[4,200,256]{2,1,0:T(8,128)S(1)}, u32[]{:S(2)}, u32[]{:S(2)}) async-start(f32[4,200,256]{2,1,0:T(8,128)} %columns.1), calls=%async_computation.2 | async-start | bytes 1638400 | tf_op jit(solution)/shard_map/all_to_all | solution.py:229
  54.3 18.6 %copy-start.4 = (s32[256]{0:T(256)S(1)}, s32[256]{0:T(256)}, u32[]{:S(2)}) copy-start(s32[256]{0:T(256)} %param.21) | copy-start | bytes 3076
  66.3 0.9 %copy-start = (f32[4,200,256]{2,1,0:T(8,128)}, f32[4,200,256]{2,1,0:T(8,128)S(1)}, u32[]{:S(2)}) copy-start(f32[4,200,256]{2,1,0:T(8,128)S(1)} %all-to-all-done.2.stack_ref) | copy-start | bytes 2457604
  69.3 12.0 %all-to-all-start.3 = ((bf16[8,40,384]{2,1,0:T(8,128)(2,1)}), bf16[8,40,384]{2,1,0:T(8,128)(2,1)S(1)}, u32[]{:S(2)}, u32[]{:S(2)}) async-start(bf16[8,40,384]{2,1,0:T(8,128)(2,1)} %bitcast.27), calls=%async_computation.3 | async-start | bytes 491520 | tf_op jit(solution)/shard_map/all_to_all | solution.py:239
  81.4 0.7 copy-start.3

commit v2 on v1

--- a/solution.py
+++ b/solution.py
@@ -11,6 +11,10 @@
 SMEM = pltpu.SMEM
 LANES = 128
 SUB = 8
+
+
+def invmem(x):
+    return pltpu.with_memory_space_constraint(x, VMEM)
 
 
 def vspec():
@@ -200,7 +204,7 @@
             in_specs=[sspec(), vspec()],
             out_specs=vspec(),
             name="select",
-        )(all_anc, held.reshape(local_rows, anc_rows + LANES))
+        )(all_anc, invmem(held.reshape(local_rows, anc_rows + LANES)))
         sub_block = lax.all_to_all(chosen, "grid", split_axis=0, concat_axis=0, tiled=True)
     else:
         shares = 1
@@ -221,7 +225,7 @@
         hpattern,
         pole_w,
         pole_z,
-        sub_block,
+        invmem(sub_block),
         factor_cols[0, 0],
         diag_inv[0, 0],
         intersection[0],
@@ -235,7 +239,7 @@
         in_specs=[vspec(), vspec()],
         out_specs=vspec(),
         name="place",
-    )(send_slot[None], stack)
+    )(send_slot[None], invmem(stack))
     arrived = lax.all_to_all(
         placed.reshape(grid_count, slots, 2 * chunk),
         "grid",
@@ -253,7 +257,7 @@
         in_specs=[vspec(), vspec()],
         out_specs=(vspec(), vspec(), sspec()),
         name="pickup",
-    )(recv_slot[None], arrived.reshape(total, 2 * chunk))
+    )(recv_slot[None], invmem(arrived.reshape(total, 2 * chunk)))
     return (density.T, energy.T, electrons[0, 0])
 
 

time: 84.5 us -> 80.8 us (0.956)
  local copies, waits for them, and re-layouts: 4.34 us -> 1.92 us
  Pallas kernels: 9.16 us -> 7.92 us
    unnamed x15 -> x7, local copies, waits for them, and re-layouts: 2.53 us -> 0.11 us
where the time goes in v2:
time: 80.8 us; the launch traced here: 80.3 us
  waiting for transfers between devices  30.8 us (38%)
  blocking collectives  24.5 us (30%)
  starting transfers between devices  10.8 us (13%)
  Pallas kernels  7.92 us (10%)
  between operations  2.67 us (3%)
  local copies, waits for them, and re-layouts  1.92 us (2%)
  other arithmetic  1.72 us (2%)
    all_to_all x1, blocking collectives, body(): held = lax.all_to_all(sent, 'grid', split_axis=0, concat_axis=0, tiled=True)  24.5 us
    all_to_all x1, waiting for transfers between devices, body(): lax.all_to_all(chosen, 'grid', split_axis=0, concat_axis=0, tiled=True)  12.1 us
    all_to_all x1, waiting for transfers between devices, body(): lax.all_to_all(stack, 'pole', split_axis=0, concat_axis=0, tiled=True)  11.1 us
    all_to_all x1, waiting for transfers between devices, body(): lax.all_to_all(placed.reshape(grid_count, slots, 2 * chunk), 'grid', spli...  7.54 us
    all_to_all x1, starting transfers between devices, body(): lax.all_to_all(placed.reshape(grid_count, slots, 2 * chunk), 'grid', spli...  3.64 us
    all_to_all x1, starting transfers between devices, body(): lax.all_to_all(stack, 'pole', split_axis=0, concat_axis=0, tiled=True)  3.63 us
    all_to_all x1, starting transfers between devices, body(): lax.all_to_all(chosen, 'grid', split_axis=0, concat_axis=0, tiled=True)  3.49 us
    pallas_call x1, Pallas kernels, body(): pl.pallas_call(functools.partial(columns_kernel, shares, chunk), out_shap...  3.01 us
  transfers between devices with their start and end apart: 3, of which 3 were waited for; matrix products, arithmetic and copies ran while one was open for 2% of the time, Pallas kernels for 0%

profile of v2, /device:TPU:0, one launch (start us, length us, event | category | flops | bytes accessed | tf_op | source)
XLA Modules:
  0.0 80.3 jit_solution(11664644293355121897)
XLA Ops:
  0.6 0.0 copy-start.2
  0.6 1.1 %copy.28 = bf16[3,8,8,1536]{3,2,0,1:T(8,128)(2,1)S(1)} copy(bf16[3,8,8,1536]{3,2,1,0:T(8,128)(2,1)} %bitcast.28) | data formatting | bytes 1179648 | tf_op jit(solution)/shard_map/reshape;squeeze | solution.py:189
  1.8 0.0 copy-done.2
  1.8 0.1 pad_maximum_fusion
  1.9 24.5 %all_to_all.20 = bf16[8,24,1664]{2,1,0:T(8,128)(2,1)S(1)} all-to-all(bf16[8,24,1664]{2,1,0:T(8,128)(2,1)S(1)} %pad_maximum_fusion), channel_id=1, replica_groups=mesh['pole'=4,'grid'=8] {'grid'}, dimensions={0} | all-to-all | bytes 1277952 | tf_op jit(solution)/shard_map/all_to_all | solution.py:196
  26.4 0.1 copy.26
  26.5 0.7 copy.25.table_ref
  27.2 1.6 %select.10 = bf16[8,64,512]{2,1,0:T(8,128)(2,1)} custom-call(s32[8,2]{1,0:T(8,128)} %copy.25.table_ref, bf16[192,1664]{1,0:T(8,128)(2,1)S(1)} %bitcast.23), custom_call_target="tpu_custom_call" | custom-call | tf_op jit(solution)/shard_map/select/pallas_call | solution.py:199
  28.8 3.5 %all-to-all-start.1 = ((bf16[8,64,512]{2,1,0:T(8,128)(2,1)}), bf16[8,64,512]{2,1,0:T(8,128)(2,1)S(1)}, u32[]{:S(2)}, u32[]{:S(2)}) async-start(bf16[8,64,512]{2,1,0:T(8,128)(2,1)} %select.10), calls=%async_computation.1 | async-start | bytes 1048576 | tf_op jit(solution)/shard_map/all_to_all | solution.py:208
  34.2 12.1 %all-to-all-done.1 = bf16[8,64,512]{2,1,0:T(8,128)(2,1)S(1)} async-done(((bf16[8,64,512]{2,1,0:T(8,128)(2,1)}), bf16[8,64,512]{2,1,0:T(8,128)(2,1)S(1)}, u32[]{:S(2)}, u32[]{:S(2)}) %all-to-all-start.1) | async-done | bytes 524320 | tf_op jit(solution)/shard_map/all_to_all | solution.py:208
  46.3 3.0 %columns.1 = f32[4,200,256]{2,1,0:T(8,128)} custom-call(s32[1]{0:T(128)S(6)} %copy.31.counts_ref, s32[1,2]{1,0:T(1,128)} %hpattern_ref.1, f32[1]{0:T(128)S(6)} %copy.29.weight_ref, f32[1]{0:T(128)S(6)} %copy.30.energy_ref, bf16[512,512]{1,0:T(8,128)(2,1)S(1)} %bitcast.24, bf16[2,256,256]{2,1,0:T(8,128)(2,1)} %bitcast.29, bf16[256,256]{1,0:T(8,128)(2,1)} %bitcast.30, ...), custom_call_target="tpu_custom_call" | custom-call | tf_op jit(solution)/shard_map/columns/pallas_call | solution.py:216
  49.4 0.0 copy-start.1
  49.4 3.6 %all-to-all-start.2 = ((f32[4,200,256]{2,1,0:T(8,128)}), f32[4,200,256]{2,1,0:T(8,128)S(1)}, u32[]{:S(2)}, u32[]{:S(2)}) async-start(f32[4,200,256]{2,1,0:T(8,128)} %columns.1), calls=%async_computation.2 | async-start | bytes 1638400 | tf_op jit(solution)/shard_map/all_to_all | solution.py:233
  53.0 0.0 copy-done.1
  53.0 0.0 copy-start
  53.0 0.2 convert_reduce_fusion
  53.2 0.6 multiply_add_fusion
  53.8 11.1 %all-to-all-done.2.stack_ref = f32[4,200,256]{2,1,0:T(8,128)S(1)} async-done(((f32[4,200,256]{2,1,0:T(8,128)}), f32[4,200,256]{2,1,0:T(8,128)S(1)}, u32[]{:S(2)}, u32[]{:S(2)}) %all-to-all-start.2) | async-done | bytes 819232 | tf_op jit(solution)/shard_map/all_to_all | solution.py:233
  64.9 1.7 %place.1 = bf16[320,384]{1,0:T(8,128)(2,1)} custom-call(s32[1,256]{1,0:T(1,128)} %bitcast.33, f32[4,200,256]{2,1,0:T(8,128)S(1)} %all-to-all-done.2.stack_ref), custom_call_target="tpu_custom_call" | custom-call | tf_op jit(solution)/shard_map/place/pallas_call | solution.py:236
  66.6 3.6 %all-to-all-start.3 = ((bf16[8,40,384]{2,1,0:T(8,128)(2,1)}), bf16[8,40,384]{2,1,0:T(8,128)(2,1)S(1)}, u32[]{:S(2)}, u32[]{:S(2)}) async-start(bf16[8,40,384]{2,1,0:T(8,128)(2,1)} %bitcast.27), calls=%async_computation.3 | async-start | bytes 491520 | tf_op jit(solution)/shard_map/all_to_all | solution.py:243
  70.3 0.0 copy-done
  70.3 0.2 convert_reduce_fusion.1
  70.5 0.6 multiply_add_fusion.1
  71.1 7.5 %all-to-all-done.3 = bf16[8,40,384]{2,1,0:T(8,128)(2,1)S(1)} async-done(((bf16[8,40,384]{2,1,0:T(8,128)(2,1)}), bf16[8,40,384]{2,1,0:T(8,128)(2,1)S(1)}, u32[]{:S(2)}, u32[]{:S(2)}) %all-to-all-start.3) | async-done | bytes 245792 | tf_op jit(solution)/shard_map/all_to_all | solution.py:243
  78.7 1.6 %pickup.1 = (bf16[192,256]{1,0:T(8,128)(2,1)}, bf16[192,256]{1,0:T(8,128)(2,1)}, f32[1,1]{1,0:T(1,128)}) custom-call(s32[1,256]{1,0:T(1,128)} %bitcast.32, bf16[320,384]{1,0:T(8,128)(2,1)S(1)} %bitcast.25), custom_call_target="tpu_custom_call" | custom-call | tf_op jit(solution)/shard_map/pickup/pallas_call | solution.py:250
  (7 shorter events, 0.1 us)
Async XLA Ops:
  0.6 1.1 %copy-start.2 = (s32[1,2]{1,0:T(1,128)S(1)}, s32[1,2]{1,0:T(1,128)}, u32[]{:S(2)}) copy-start(s32[1,2]{1,0:T(1,128)} %param.17) | copy-start | bytes 28
  28.8 17.6 %all-to-all-start.1 = ((bf16[8,64,512]{2,1,0:T(8,128)(2,1)}), bf16[8,64,512]{2,1,0:T(8,128)(2,1)S(1)}, u32[]{:S(2)}, u32[]{:S(2)}) async-start(bf16[8,64,512]{2,1,0:T(8,128)(2,1)} %select.10), calls=%async_computation.1 | async-start | bytes 1048576 | tf_op jit(solution)/shard_map/all_to_all | solution.py:208
  49.4 3.6 %copy-start.1 = (s32[256]{0:T(256)S(1)}, s32[256]{0:T(256)}, u32[]{:S(2)}) copy-start(s32[256]{0:T(256)} %param.20) | copy-start | bytes 3076
  49.4 15.6 %all-to-all-start.2 = ((f32[4,200,256]{2,1,0:T(8,128)}), f32[4,200,256]{2,1,0:T(8,128)S(1)}, u32[]{:S(2)}, u32[]{:S(2)}) async-start(f32[4,200,256]{2,1,0:T(8,128)} %columns.1), calls=%async_computation.2 | async-start | bytes 1638400 | tf_op jit(solution)/shard_map/all_to_all | solution.py:233
  53.0 17.3 %copy-start = (s32[256]{0:T(256)S(1)}, s32[256]{0:T(256)}, u32[]{:S(2)}) copy-start(s32[256]{0:T(256)} %param.21) | copy-start | bytes 3076
  66.6 12.0 %all-to-all-start.3 = ((bf16[8,40,384]{2,1,0:T(8,128)(2,1)}), bf16[8,40,384]{2,1,0:T(8,128)(2,1)S(1)}, u32[]{:S(2)}, u32[]{:S(2)}) async-start(bf16[8,40,384]{2,1,0:T(8,128)(2,1)} %bitcast.27), calls=%async_computation.3 | async-start | bytes 491520 | tf_op jit(solution)/shard_map/all_to_all | solution.py:243

commit v3 on v2

--- a/solution.py
+++ b/solution.py
@@ -11,6 +11,9 @@
 SMEM = pltpu.SMEM
 LANES = 128
 SUB = 8
+TINY = 1e-30
+FINE = 64.0
+STEPS = 32760.0
 
 
 def invmem(x):
@@ -150,6 +153,208 @@
     count_ref[0, 0] = jnp.sum(pieces)
 
 
+def order_kernel(
+    counts_ref, slot_ref, factor_ref, diag_ref, inter_ref, lower_ref, turned_ref, diag_out, inter_out
+):
+    blk_count, width, _ = factor_ref.shape
+    one_hot = (lax.broadcasted_iota(jnp.int32, (width, width), 0) == slot_ref[...]).astype(
+        jnp.bfloat16
+    )
+
+    def turn(matrix):
+        return lax.dot_general(
+            one_hot, matrix, (((1,), (1,)), ((), ())), preferred_element_type=jnp.float32
+        ).astype(jnp.bfloat16)
+
+    for m in range(blk_count):
+        live = (m < counts_ref[0]).astype(jnp.float32).astype(jnp.bfloat16)
+        block = factor_ref[m] * live
+        lower_ref[m * width : (m + 1) * width, :] = block
+        turned_ref[:, m * width : (m + 1) * width] = turn(block)
+    diag_out[...] = turn(diag_ref[...])
+    inter_out[...] = turn(inter_ref[...])
+
+
+def halved_sum(values):
+    while values.shape[0] > SUB:
+        half = values.shape[0] // 2
+        values = values[:half] + values[half:]
+    while values.shape[1] > LANES:
+        half = values.shape[1] // 2
+        values = values[:, :half] + values[:, half:]
+    return jnp.sum(values)
+
+
+def whole(value):
+    return value.astype(jnp.int32).astype(jnp.int16)
+
+
+def fold_half(tile, right):
+    rows = tile.shape[0] // 2
+    lane = lax.broadcasted_iota(jnp.int32, (rows, LANES), 1)
+    top, bottom = tile[:rows], tile[rows:]
+    if right:
+        return jnp.where(lane < LANES // 2, pltpu.roll(top, LANES // 2, 1), bottom)
+    return jnp.where(lane < LANES // 2, top, pltpu.roll(bottom, LANES // 2, 1))
+
+
+def encode_kernel(
+    shares,
+    chunk,
+    hpattern_ref,
+    weight_ref,
+    energy_ref,
+    rows_ref,
+    lower_ref,
+    turned_ref,
+    diag_ref,
+    inter_ref,
+    out_ref,
+    sorted_ref,
+):
+    blk_count = hpattern_ref.shape[1]
+    width = lower_ref.shape[1]
+    per_blk = width // shares
+    for m in range(blk_count):
+        for j in range(shares):
+            at = (j * blk_count + m) * per_blk
+            piece = rows_ref[at : at + per_blk, :].astype(jnp.float32)
+            for c in range(per_blk // SUB):
+                row = m * width + (c * shares + j) * SUB
+                sorted_ref[row : row + SUB, :] = piece[c * SUB : (c + 1) * SUB]
+    off = -lax.dot_general(
+        turned_ref[...],
+        sorted_ref[...].astype(jnp.bfloat16),
+        (((1,), (1,)), ((), ())),
+        preferred_element_type=jnp.float32,
+    )
+    high = off.astype(jnp.bfloat16)
+    rest = off - high.astype(jnp.float32)
+    mid = rest.astype(jnp.bfloat16)
+    low = (rest - mid.astype(jnp.float32)).astype(jnp.bfloat16)
+    lower = lower_ref[...]
+    diag = diag_ref[...].astype(jnp.float32) - (
+        jnp.dot(low, lower, preferred_element_type=jnp.float32)
+        + jnp.dot(mid, lower, preferred_element_type=jnp.float32)
+        + jnp.dot(high, lower, preferred_element_type=jnp.float32)
+    )
+    count = weight_ref[0] * halved_sum(diag * inter_ref[...].astype(jnp.float32))
+    parts = [diag] + [
+        off[:, m * width : (m + 1) * width] * hpattern_ref[0, m].astype(jnp.float32)
+        for m in range(blk_count)
+    ]
+    values = jnp.concatenate(parts, axis=1)
+    largest = jnp.max(jnp.abs(values), axis=0, keepdims=True)
+    level = jnp.ceil(jnp.log2(jnp.maximum(largest, TINY)) * FINE)
+    codes = jnp.floor(values * (jnp.exp2(level * (-1.0 / FINE)) * STEPS) + 0.5)
+
+    row_id = lax.broadcasted_iota(jnp.int32, (SUB, LANES), 0)
+    lane_id = lax.broadcasted_iota(jnp.int32, (SUB, LANES), 1)
+    full_count = jnp.full((SUB, LANES), count)
+    power = jnp.ceil(jnp.log2(jnp.maximum(jnp.abs(full_count), TINY)))
+    scaled = full_count * jnp.exp2(-power) * 2.0**14
+    scaled_high = jnp.floor(scaled)
+    extra = jnp.where(
+        lane_id == 0,
+        power,
+        jnp.where(lane_id == 1, scaled_high, jnp.floor((scaled - scaled_high) * 2.0**15)),
+    )
+    for at, scalar in ((2, weight_ref[0]), (4, energy_ref[0])):
+        grown = jnp.full((SUB, LANES), scalar) * 2.0**13
+        grown_high = jnp.floor(grown)
+        extra = jnp.where(row_id == at, grown_high, extra)
+        extra = jnp.where(row_id == at + 1, (grown - grown_high) * 2.0**15, extra)
+
+    dests, _, _ = out_ref.shape
+    pole_count = values.shape[1] // chunk
+    owners = dests // pole_count
+    cap = width // owners
+    half = cap // 2
+    for q in range(pole_count):
+        right = q % 2 == 1
+        full_at = (q * chunk + LANES - 1) // LANES * LANES
+        half_at = full_at - LANES if right else full_at + LANES
+        level_half = level[:, half_at : half_at + LANES]
+        lane = lax.broadcasted_iota(jnp.int32, (1, LANES), 1)
+        other = pltpu.roll(jnp.broadcast_to(level_half, (SUB, LANES)), LANES // 2, 1)[:1]
+        level_half = jnp.where((lane < LANES // 2) == (not right), level_half, other)
+        tail = jnp.where(
+            row_id == 0,
+            level[:, full_at : full_at + LANES],
+            jnp.where(row_id == 1, level_half, extra),
+        )
+        tail = whole(tail)
+        for g in range(owners):
+            rows = slice(g * cap, (g + 1) * cap)
+            d = q * owners + g
+            out_ref[d, :cap, :] = whole(codes[rows, full_at : full_at + LANES])
+            out_ref[d, cap : cap + half, :] = whole(
+                fold_half(codes[rows, half_at : half_at + LANES], right)
+            )
+            out_ref[d, cap + half :, :] = tail
+
+
+def decode_kernel(
+    owners, cap, odd_ref, slot_ref, recv_ref, dens_ref, energy_ref, count_ref, full_ref, half_ref
+):
+    dests, rows, _ = recv_ref.shape
+    poles = dests // owners
+    half = cap // 2
+    width = slot_ref.shape[1]
+    count = jnp.zeros((1, 1), jnp.float32)
+    lost = jnp.zeros((1, 1), jnp.float32)
+    for g in range(owners):
+        sums = [0.0, 0.0, 0.0, 0.0]
+        for p in range(poles):
+            piece = recv_ref[p * owners + g].astype(jnp.int32).astype(jnp.float32)
+            extra = piece[cap + half :]
+            scale = jnp.exp2(extra[:2] * (1.0 / FINE)) * (1.0 / STEPS)
+            weight = extra[2:3] * 2.0**-13 + extra[3:4] * 2.0**-28
+            energy = extra[4:5] * 2.0**-13 + extra[5:6] * 2.0**-28
+            full = piece[:cap] * scale[:1]
+            rest = piece[cap : cap + half] * scale[1:2]
+            for at, term in enumerate(
+                (weight * full, energy * full, weight * rest, energy * rest)
+            ):
+                sums[at] = sums[at] + term
+            own = extra[6:7]
+            own = (own[:, 1:2] * 2.0**-14 + own[:, 2:3] * 2.0**-29) * jnp.exp2(own[:, 0:1])
+            grown = count + own
+            part = grown - count
+            lost = lost + ((count - (grown - part)) + (own - part))
+            count = grown
+        full_ref[g * cap : (g + 1) * cap, :LANES] = sums[0].astype(jnp.bfloat16)
+        full_ref[g * cap : (g + 1) * cap, LANES:] = sums[1].astype(jnp.bfloat16)
+        half_ref[g * half : (g + 1) * half, :LANES] = sums[2].astype(jnp.bfloat16)
+        half_ref[g * half : (g + 1) * half, LANES:] = sums[3].astype(jnp.bfloat16)
+    count_ref[0, 0] = jnp.sum(count + lost)
+
+    slot = slot_ref[...]
+    pick = (lax.broadcasted_iota(jnp.int32, (owners * cap, width), 0) == slot).astype(jnp.bfloat16)
+    row = lax.broadcasted_iota(jnp.int32, (owners * half, width), 0)
+    owner = slot // cap
+    within = slot - owner * cap
+    place = owner * half + within
+    left = (row == jnp.where(within < half, place, -1)).astype(jnp.bfloat16)
+    right = (row == jnp.where(within >= half, place - half, -1)).astype(jnp.bfloat16)
+
+    def take(held, chosen):
+        return lax.dot_general(
+            held, chosen, (((0,), (0,)), ((), ())), preferred_element_type=jnp.float32
+        )
+
+    full = take(full_ref[...], pick).astype(jnp.bfloat16)
+    by_left = take(half_ref[...], left)
+    by_right = take(half_ref[...], right)
+    mid = LANES // 2
+    full_at = pl.multiple_of(odd_ref[0] * mid, mid)
+    half_at = pl.multiple_of((1 - odd_ref[0]) * LANES, mid)
+    for at, ref in ((0, dens_ref), (LANES, energy_ref)):
+        ref[pl.ds(full_at, LANES), :] = full[at : at + LANES]
+        joined = by_left[at : at + mid] + by_right[at + mid : at + LANES]
+        ref[pl.ds(half_at, mid), :] = joined.astype(jnp.bfloat16)
+
+
 def ranks(own, order):
     same = own[:, None] == own[None, :]
     earlier = order[None, :] < order[:, None]
@@ -176,7 +381,10 @@
     pole_count = lax.axis_size("pole")
     chunk = (blk_count + 1) * width // pole_count
     slot_cap = (width + grid_count - 1) // grid_count
-    slots = slot_cap + (SUB if slot_cap % SUB == 0 else 1)
+    direct = (
+        slot_cap * grid_count == width and slot_cap % 32 == 0 and chunk == LANES * 3 // 2
+    )
+    slots = slot_cap + (0 if direct else SUB if slot_cap % SUB == 0 else 1)
 
     dest_owner = siesta_of // width
     send_slot = dest_owner * slots + ranks(dest_owner, jnp.arange(width))
@@ -213,6 +421,48 @@
         sub_block = jnp.take(jnp.take(blocks, ancestors[0], axis=0), ancestors[0], axis=2)
     sub_block = sub_block.reshape(blk_count * width, blk_count * width)
 
+    if direct:
+        factor, diag, inter = factor_cols[0, 0], diag_inv[0, 0], intersection[0]
+        square = jax.ShapeDtypeStruct((width, width), jnp.bfloat16)
+        lower, turned, diag, inter = pl.pallas_call(
+            order_kernel,
+            out_shape=(
+                jax.ShapeDtypeStruct((blk_count * width, width), jnp.bfloat16),
+                jax.ShapeDtypeStruct((width, blk_count * width), jnp.bfloat16),
+                square,
+                square,
+            ),
+            in_specs=[sspec()] + [vspec()] * 4,
+            out_specs=(vspec(),) * 4,
+            name="order",
+        )(counts, send_slot[None], factor, diag, inter)
+        rows = slot_cap * 3 // 2 + SUB
+        coded = pl.pallas_call(
+            functools.partial(encode_kernel, shares, chunk),
+            out_shape=jax.ShapeDtypeStruct((pole_count * grid_count, rows, LANES), jnp.int16),
+            in_specs=[sspec()] * 3 + [vspec()] * 5,
+            out_specs=vspec(),
+            scratch_shapes=[VMEM((blk_count * width, blk_count * width), jnp.float32)],
+            name="encode",
+        )(hpattern, pole_w, pole_z, invmem(sub_block), *map(invmem, (lower, turned, diag, inter)))
+        arrived = lax.all_to_all(
+            coded, ("pole", "grid"), split_axis=0, concat_axis=0, tiled=True
+        )
+        odd = (lax.axis_index("pole") & 1).astype(jnp.int32)[None]
+        half = jax.ShapeDtypeStruct((chunk, width), jnp.bfloat16)
+        density, energy, electrons = pl.pallas_call(
+            functools.partial(decode_kernel, grid_count, slot_cap),
+            out_shape=(half, half, jax.ShapeDtypeStruct((1, 1), jnp.float32)),
+            in_specs=[sspec(), vspec(), vspec()],
+            out_specs=(vspec(), vspec(), sspec()),
+            scratch_shapes=[
+                VMEM((width, 2 * LANES), jnp.bfloat16),
+                VMEM((width // 2, 2 * LANES), jnp.bfloat16),
+            ],
+            name="decode",
+        )(odd, recv_slot[None], invmem(arrived))
+        return (density.T, energy.T, electrons[0, 0])
+
     stack = pl.pallas_call(
         functools.partial(columns_kernel, shares, chunk),
         out_shape=jax.ShapeDtypeStruct((pole_count, chunk + SUB, width), jnp.float32),

time: 80.8 us -> 74.3 us (0.920)
  waiting for transfers between devices: 30.8 us -> 23.2 us
  local copies, waits for them, and re-layouts: 1.92 us -> 5.61 us
  starting transfers between devices: 10.8 us -> 7.27 us
    all_to_all x2 -> x1, waiting for transfers between devices: 18.7 us -> 14 us  [body(): lax.all_to_all(coded, ('pole', 'grid'), split_axis=0, concat_axis=0, tile...]
    unnamed x7 -> x13, local copies, waits for them, and re-layouts: 0.11 us -> 3.81 us
    all_to_all x2 -> x1, starting transfers between devices: 7.26 us -> 3.65 us  [body(): lax.all_to_all(coded, ('pole', 'grid'), split_axis=0, concat_axis=0, tile...]
    all_to_all x1, waiting for transfers between devices: 12.1 us -> 9.2 us  [body(): lax.all_to_all(chosen, 'grid', split_axis=0, concat_axis=0, tiled=True)]
  transfers between devices with their start and end apart: 3 -> 2, of which waited for: 3 -> 2; matrix products, arithmetic and copies ran while one was open for 2% -> 2% of each run, Pallas kernels for 0% -> 3%
where the time goes in v3:
time: 74.3 us; the launch traced here: 73.7 us
  blocking collectives  24.5 us (33%)
  waiting for transfers between devices  23.2 us (31%)
  Pallas kernels  8.09 us (11%)
  starting transfers between devices  7.27 us (10%)
  local copies, waits for them, and re-layouts  5.61 us (8%)
  between operations  2.65 us (4%)
  other arithmetic  2.33 us (3%)
    all_to_all x1, blocking collectives, body(): held = lax.all_to_all(sent, 'grid', split_axis=0, concat_axis=0, tiled=True)  24.5 us
    all_to_all x1, waiting for transfers between devices, body(): lax.all_to_all(coded, ('pole', 'grid'), split_axis=0, concat_axis=0, tile...  14 us
    all_to_all x1, waiting for transfers between devices, body(): lax.all_to_all(chosen, 'grid', split_axis=0, concat_axis=0, tiled=True)  9.2 us
    unnamed x13, local copies, waits for them, and re-layouts  3.81 us
    all_to_all x1, starting transfers between devices, body(): lax.all_to_all(coded, ('pole', 'grid'), split_axis=0, concat_axis=0, tile...  3.65 us
    all_to_all x1, starting transfers between devices, body(): lax.all_to_all(chosen, 'grid', split_axis=0, concat_axis=0, tiled=True)  3.62 us
    pallas_call x1, Pallas kernels, body(): pl.pallas_call(functools.partial(encode_kernel, shares, chunk), out_shape...  2.52 us
    pallas_call x1, Pallas kernels, body(): pl.pallas_call(order_kernel, out_shape=(jax.ShapeDtypeStruct((blk_count *...  2.14 us
  transfers between devices with their start and end apart: 2, of which 2 were waited for; matrix products, arithmetic and copies ran while one was open for 2% of the time, Pallas kernels for 3%

profile of v3, /device:TPU:0, one launch (start us, length us, event | category | flops | bytes accessed | tf_op | source)
XLA Modules:
  0.0 73.7 jit_solution(145343227665243477)
XLA Ops:
  0.6 0.7 convert.5
  1.3 1.1 %copy.28 = bf16[3,8,8,1536]{3,2,0,1:T(8,128)(2,1)S(1)} copy(bf16[3,8,8,1536]{3,2,1,0:T(8,128)(2,1)} %bitcast.25) | data formatting | bytes 1179648 | tf_op jit(solution)/shard_map/reshape;squeeze | solution.py:397
  2.4 0.1 pad_maximum_fusion
  2.5 24.5 %all_to_all.15 = bf16[8,24,1664]{2,1,0:T(8,128)(2,1)S(1)} all-to-all(bf16[8,24,1664]{2,1,0:T(8,128)(2,1)S(1)} %pad_maximum_fusion), channel_id=1, replica_groups=mesh['pole'=4,'grid'=8] {'grid'}, dimensions={0} | all-to-all | bytes 1277952 | tf_op jit(solution)/shard_map/all_to_all | solution.py:404
  27.0 0.1 copy.26
  27.1 0.7 copy.25.table_ref
  27.8 1.6 %select.10 = bf16[8,64,512]{2,1,0:T(8,128)(2,1)} custom-call(s32[8,2]{1,0:T(8,128)} %copy.25.table_ref, bf16[192,1664]{1,0:T(8,128)(2,1)S(1)} %bitcast.22), custom_call_target="tpu_custom_call" | custom-call | tf_op jit(solution)/shard_map/select/pallas_call | solution.py:407
  29.4 0.0 copy-start.5
  29.4 3.6 %all-to-all-start.1 = ((bf16[8,64,512]{2,1,0:T(8,128)(2,1)}), bf16[8,64,512]{2,1,0:T(8,128)(2,1)S(1)}, u32[]{:S(2)}, u32[]{:S(2)}) async-start(bf16[8,64,512]{2,1,0:T(8,128)(2,1)} %select.10), calls=%async_computation.1 | async-start | bytes 1048576 | tf_op jit(solution)/shard_map/all_to_all | solution.py:416
  35.0 0.0 copy-done.5
  35.0 0.2 convert_reduce_fusion
  35.2 0.6 multiply_add_fusion
  35.7 2.1 %order.1 = (bf16[512,256]{1,0:T(8,128)(2,1)}, bf16[256,512]{1,0:T(8,128)(2,1)}, bf16[256,256]{1,0:T(8,128)(2,1)}, bf16[256,256]{1,0:T(8,128)(2,1)}) custom-call(s32[1]{0:T(128)S(6)} %copy.31.counts_ref, s32[1,256]{1,0:T(1,128)} %bitcast.30, bf16[2,256,256]{2,1,0:T(8,128)(2,1)} %bitcast.26, bf16[256,256]{1,0:T(8,128)(2,1)} %bitcast.27, bf16[256,256]{1,0:T(8,128)(2,1)} %bitcast.28), custom_call_target="tpu_custom_call" | custom-call | tf_op jit(solution)/shard_map/order/pallas_call | solution.py:427
  37.9 9.2 %all-to-all-done.1 = bf16[8,64,512]{2,1,0:T(8,128)(2,1)S(1)} async-done(((bf16[8,64,512]{2,1,0:T(8,128)(2,1)}), bf16[8,64,512]{2,1,0:T(8,128)(2,1)S(1)}, u32[]{:S(2)}, u32[]{:S(2)}) %all-to-all-start.1) | async-done | bytes 524320 | tf_op jit(solution)/shard_map/all_to_all | solution.py:416
  47.1 0.0 copy-start
  47.1 0.9 %copy-done = bf16[512,256]{1,0:T(8,128)(2,1)S(1)} copy-done((bf16[512,256]{1,0:T(8,128)(2,1)S(1)}, bf16[512,256]{1,0:T(8,128)(2,1)}, u32[]{:S(2)}) %copy-start) | copy-done | bytes 262168
  48.0 0.0 copy-start.1
  48.0 0.9 %copy-done.1 = bf16[256,512]{1,0:T(8,128)(2,1)S(1)} copy-done((bf16[256,512]{1,0:T(8,128)(2,1)S(1)}, bf16[256,512]{1,0:T(8,128)(2,1)}, u32[]{:S(2)}) %copy-start.1) | copy-done | bytes 262168
  49.0 0.0 copy-start.2
  49.0 0.9 %copy-done.2 = bf16[256,256]{1,0:T(8,128)(2,1)S(1)} copy-done((bf16[256,256]{1,0:T(8,128)(2,1)S(1)}, bf16[256,256]{1,0:T(8,128)(2,1)}, u32[]{:S(2)}) %copy-start.2) | copy-done | bytes 131096
  49.9 0.0 copy-start.3
  49.9 0.9 %copy-done.3 = bf16[256,256]{1,0:T(8,128)(2,1)S(1)} copy-done((bf16[256,256]{1,0:T(8,128)(2,1)S(1)}, bf16[256,256]{1,0:T(8,128)(2,1)}, u32[]{:S(2)}) %copy-start.3) | copy-done | bytes 131096
  50.8 2.5 %encode.1 = s16[32,56,128]{2,1,0:T(8,128)(2,1)} custom-call(s32[1,2]{1,0:T(1,128)} %hpattern_ref.1, f32[1]{0:T(128)S(6)} %copy.29.weight_ref, f32[1]{0:T(128)S(6)} %copy.30.energy_ref, bf16[512,512]{1,0:T(8,128)(2,1)S(1)} %bitcast.23, bf16[512,256]{1,0:T(8,128)(2,1)S(1)} %copy-done, bf16[256,512]{1,0:T(8,128)(2,1)S(1)} %copy-done.1, ...), custom_call_target="tpu_custom_call" | custom-call | tf_op jit(solution)/shard_map/encode/pallas_call | solution.py:440
  53.3 0.0 copy-start.4
  53.3 3.7 %all-to-all-start.2 = ((s16[32,56,128]{2,1,0:T(8,128)(2,1)}), s16[32,56,128]{2,1,0:T(8,128)(2,1)S(1)}, u32[]{:S(2)}, u32[]{:S(2)}) async-start(s16[32,56,128]{2,1,0:T(8,128)(2,1)} %encode.1), calls=%async_computation.2 | async-start | bytes 917504 | tf_op jit(solution)/shard_map/all_to_all | solution.py:448
  57.0 0.0 copy-done.4
  57.0 0.2 convert_reduce_fusion.1
  57.2 0.6 multiply_add_fusion.1
  57.8 14.0 %all-to-all-done.2.recv_ref = s16[32,56,128]{2,1,0:T(8,128)(2,1)S(1)} async-done(((s16[32,56,128]{2,1,0:T(8,128)(2,1)}), s16[32,56,128]{2,1,0:T(8,128)(2,1)S(1)}, u32[]{:S(2)}, u32[]{:S(2)}) %all-to-all-start.2) | async-done | bytes 458784 | tf_op jit(solution)/shard_map/all_to_all | solution.py:448
  71.8 1.9 %decode.1 = (bf16[192,256]{1,0:T(8,128)(2,1)}, bf16[192,256]{1,0:T(8,128)(2,1)}, f32[1,1]{1,0:T(1,128)}) custom-call(s32[1]{0:T(128)} %bitcast.odd_ref, s32[1,256]{1,0:T(1,128)} %bitcast.29, s16[32,56,128]{2,1,0:T(8,128)(2,1)S(1)} %all-to-all-done.2.recv_ref), custom_call_target="tpu_custom_call" | custom-call | tf_op jit(solution)/shard_map/decode/pallas_call | solution.py:453
  (6 shorter events, 0.0 us)
Async XLA Ops:
  29.4 5.6 %copy-start.5 = (s32[256]{0:T(256)S(1)}, s32[256]{0:T(256)}, u32[]{:S(2)}) copy-start(s32[256]{0:T(256)} %param.20) | copy-start | bytes 3076
  29.4 17.7 %all-to-all-start.1 = ((bf16[8,64,512]{2,1,0:T(8,128)(2,1)}), bf16[8,64,512]{2,1,0:T(8,128)(2,1)S(1)}, u32[]{:S(2)}, u32[]{:S(2)}) async-start(bf16[8,64,512]{2,1,0:T(8,128)(2,1)} %select.10), calls=%async_computation.1 | async-start | bytes 1048576 | tf_op jit(solution)/shard_map/all_to_all | solution.py:416
  47.1 1.0 %copy-start = (bf16[512,256]{1,0:T(8,128)(2,1)S(1)}, bf16[512,256]{1,0:T(8,128)(2,1)}, u32[]{:S(2)}) copy-start(bf16[512,256]{1,0:T(8,128)(2,1)} %get-tuple-element.10.lower_ref) | copy-start | bytes 786436
  48.0 0.9 %copy-start.1 = (bf16[256,512]{1,0:T(8,128)(2,1)S(1)}, bf16[256,512]{1,0:T(8,128)(2,1)}, u32[]{:S(2)}) copy-start(bf16[256,512]{1,0:T(8,128)(2,1)} %get-tuple-element.11.turned_ref) | copy-start | bytes 786436
  49.0 0.9 %copy-start.2 = (bf16[256,256]{1,0:T(8,128)(2,1)S(1)}, bf16[256,256]{1,0:T(8,128)(2,1)}, u32[]{:S(2)}) copy-start(bf16[256,256]{1,0:T(8,128)(2,1)} %get-tuple-element.12.diag_ref) | copy-start | bytes 393220
  49.9 0.9 %copy-start.3 = (bf16[256,256]{1,0:T(8,128)(2,1)S(1)}, bf16[256,256]{1,0:T(8,128)(2,1)}, u32[]{:S(2)}) copy-start(bf16[256,256]{1,0:T(8,128)(2,1)} %get-tuple-element.13.inter_ref) | copy-start | bytes 393220
  53.3 3.7 %copy-start.4 = (s32[256]{0:T(256)S(1)}, s32[256]{0:T(256)}, u32[]{:S(2)}) copy-start(s32[256]{0:T(256)} %param.21) | copy-start | bytes 3076
  53.3 18.5 %all-to-all-start.2 = ((s16[32,56,128]{2,1,0:T(8,128)(2,1)}), s16[32,56,128]{2,1,0:T(8,128)(2,1)S(1)}, u32[]{:S(2)}, u32[]{:S(2)}) async-start(s16[32,56,128]{2,1,0:T(8,128)(2,1)} %encode.1), calls=%async_computation.2 | async-start | bytes 917504 | tf_op jit(solution)/shard_map/all_to_all | solution.py:448

commit v4 on v3

--- a/solution.py
+++ b/solution.py
@@ -24,21 +24,61 @@
     return pl.BlockSpec(memory_space=VMEM)
 
 
+def hspec():
+    return pl.BlockSpec(memory_space=pltpu.HBM)
+
+
 def sspec():
     return pl.BlockSpec(memory_space=SMEM)
 
 
-def select_kernel(width, rows, blk_count, table_ref, spread_ref, out_ref):
-    for dest in range(out_ref.shape[0]):
-        for row_blk in range(blk_count):
-            row_at = pl.multiple_of(table_ref[dest, row_blk] * rows, rows)
-            for col_blk in range(blk_count):
-                col_at = pl.multiple_of(table_ref[dest, col_blk] * width, width)
-                out_ref[
-                    dest,
-                    row_blk * rows : (row_blk + 1) * rows,
-                    col_blk * width : (col_blk + 1) * width,
-                ] = spread_ref[pl.ds(row_at, rows), pl.ds(col_at, width)]
+def pack_kernel(table_ref, rows_ref, out_ref, sems):
+    stretches, _, _, width = rows_ref.shape
+    copies = [
+        pltpu.make_async_copy(
+            rows_ref.at[c], out_ref.at[:, c * SUB : (c + 1) * SUB, :width], sems.at[c]
+        )
+        for c in range(stretches)
+    ]
+    for copy in copies:
+        copy.start()
+    shares, rows, lanes = out_ref.shape
+    lane = lax.broadcasted_iota(jnp.int32, (rows, lanes - width), 1)
+    table = jnp.zeros((rows, lanes - width), jnp.float32)
+    for m in range(table_ref.shape[1]):
+        table = jnp.where(lane == m, table_ref[0, m].astype(jnp.float32), table)
+    table = table.astype(jnp.bfloat16)
+    for j in range(shares):
+        out_ref[j, :, width:] = table
+    for copy in copies:
+        copy.wait()
+
+
+def select_kernel(width, blk_count, held_ref, out_ref, sems):
+    dests, picked, _ = out_ref.shape
+    rows = picked // blk_count
+    local = held_ref.shape[0] // dests
+    tail = held_ref.shape[1] - LANES
+    lane = lax.broadcasted_iota(jnp.int32, (1, LANES), 1)
+    copies = []
+    for dest in range(dests):
+        entry = held_ref[dest * local : (dest + 1) * local, tail:].astype(jnp.float32)[:1]
+        table = [
+            jnp.sum(jnp.where(lane == m, entry, 0.0)).astype(jnp.int32) for m in range(blk_count)
+        ]
+        for m in range(blk_count):
+            row_at = pl.multiple_of(table[m] * rows, rows)
+            for n in range(blk_count):
+                col_at = pl.multiple_of(table[n] * width, width)
+                copy = pltpu.make_async_copy(
+                    held_ref.at[pl.ds(row_at, rows), pl.ds(col_at, width)],
+                    out_ref.at[dest, m * rows : (m + 1) * rows, n * width : (n + 1) * width],
+                    sems.at[dest, m, n],
+                )
+                copy.start()
+                copies.append(copy)
+    for copy in copies:
+        copy.wait()
 
 
 def columns_kernel(
@@ -394,25 +434,28 @@
     spread = grid_count * SUB
     if local_rows % spread == 0 and width % spread == 0:
         shares = grid_count
-        mine = anc_inv[0].reshape(local_rows // spread, grid_count, SUB, anc_rows)
-        mine = mine.transpose(1, 0, 2, 3).reshape(grid_count, local_rows // grid_count, anc_rows)
-        table = jnp.broadcast_to(
-            jnp.pad(ancestors, ((0, 0), (0, LANES - blk_count))).astype(jnp.bfloat16)[None],
-            (grid_count, local_rows // grid_count, LANES),
-        )
-        sent = jnp.concatenate([mine, table], axis=2)
+        stretches = local_rows // spread
+        sent = pl.pallas_call(
+            pack_kernel,
+            out_shape=VMEM(
+                (grid_count, local_rows // grid_count, anc_rows + LANES), jnp.bfloat16
+            ),
+            in_specs=[sspec(), hspec()],
+            scratch_shapes=[pltpu.SemaphoreType.DMA((stretches,))],
+            name="pack",
+        )(ancestors, anc_inv[0].reshape(stretches, grid_count, SUB, anc_rows))
         held = lax.all_to_all(sent, "grid", split_axis=0, concat_axis=0, tiled=True)
-        all_anc = held[:, 0, anc_rows : anc_rows + blk_count].astype(jnp.int32)
         rows = width // grid_count
         chosen = pl.pallas_call(
-            functools.partial(select_kernel, width, rows, blk_count),
+            functools.partial(select_kernel, width, blk_count),
             out_shape=jax.ShapeDtypeStruct(
                 (grid_count, blk_count * rows, blk_count * width), jnp.bfloat16
             ),
-            in_specs=[sspec(), vspec()],
-            out_specs=vspec(),
+            in_specs=[vspec()],
+            out_specs=hspec(),
+            scratch_shapes=[pltpu.SemaphoreType.DMA((grid_count, blk_count, blk_count))],
             name="select",
-        )(all_anc, invmem(held.reshape(local_rows, anc_rows + LANES)))
+        )(invmem(held.reshape(local_rows, anc_rows + LANES)))
         sub_block = lax.all_to_all(chosen, "grid", split_axis=0, concat_axis=0, tiled=True)
     else:
         shares = 1
@@ -427,13 +470,12 @@
         lower, turned, diag, inter = pl.pallas_call(
             order_kernel,
             out_shape=(
-                jax.ShapeDtypeStruct((blk_count * width, width), jnp.bfloat16),
-                jax.ShapeDtypeStruct((width, blk_count * width), jnp.bfloat16),
-                square,
-                square,
+                VMEM((blk_count * width, width), jnp.bfloat16),
+                VMEM((width, blk_count * width), jnp.bfloat16),
+                VMEM((width, width), jnp.bfloat16),
+                VMEM((width, width), jnp.bfloat16),
             ),
             in_specs=[sspec()] + [vspec()] * 4,
-            out_specs=(vspec(),) * 4,
             name="order",
         )(counts, send_slot[None], factor, diag, inter)
         rows = slot_cap * 3 // 2 + SUB

time: 74.3 us -> 69.1 us (0.930)
  local copies, waits for them, and re-layouts: 5.61 us -> 0.69 us
  other arithmetic: 2.33 us -> 1.55 us
    unnamed x13 -> x4, local copies, waits for them, and re-layouts: 3.81 us -> 0.69 us
    another operation x1 -> x0, local copies, waits for them, and re-layouts: 1.1 us -> none  [body(): mine = anc_inv[0].reshape(local_rows // spread, grid_count, SUB, anc_rows)]
    pallas_call x2 -> x3, Pallas kernels: 3.71 us -> 4.44 us  [the longest x1 1.8 us: body(): pl.pallas_call(pack_kernel, out_shape=VMEM((grid_count, local_rows // gri...]
  transfers between devices with their start and end apart: 2 -> 2, of which waited for: 2 -> 2; matrix products, arithmetic and copies ran while one was open for 2% -> 2% of each run, Pallas kernels for 3% -> 2%
where the time goes in v4:
time: 69.1 us; the launch traced here: 68.6 us
  blocking collectives  24.5 us (35%)
  waiting for transfers between devices  23.3 us (34%)
  Pallas kernels  8.83 us (13%)
  starting transfers between devices  7.15 us (10%)
  between operations  2.65 us (4%)
  other arithmetic  1.55 us (2%)
    all_to_all x1, blocking collectives, body(): held = lax.all_to_all(sent, 'grid', split_axis=0, concat_axis=0, tiled=True)  24.5 us
    all_to_all x1, waiting for transfers between devices, body(): lax.all_to_all(coded, ('pole', 'grid'), split_axis=0, concat_axis=0, tile...  13.4 us
    all_to_all x1, waiting for transfers between devices, body(): lax.all_to_all(chosen, 'grid', split_axis=0, concat_axis=0, tiled=True)  9.91 us
    all_to_all x1, starting transfers between devices, body(): lax.all_to_all(coded, ('pole', 'grid'), split_axis=0, concat_axis=0, tile...  3.65 us
    all_to_all x1, starting transfers between devices, body(): lax.all_to_all(chosen, 'grid', split_axis=0, concat_axis=0, tiled=True)  3.5 us
    pallas_call x1, Pallas kernels, body(): pl.pallas_call(functools.partial(encode_kernel, shares, chunk), out_shape...  2.52 us
    pallas_call x1, Pallas kernels, body(): pl.pallas_call(functools.partial(decode_kernel, grid_count, slot_cap), ou...  1.86 us
    pallas_call x1, Pallas kernels, body(): pl.pallas_call(pack_kernel, out_shape=VMEM((grid_count, local_rows // gri...  1.8 us
  transfers between devices with their start and end apart: 2, of which 2 were waited for; matrix products, arithmetic and copies ran while one was open for 2% of the time, Pallas kernels for 2%

profile of v4, /device:TPU:0, one launch (start us, length us, event | category | flops | bytes accessed | tf_op | source)
XLA Modules:
  0.0 68.6 jit_solution(7939864965043010173)
XLA Ops:
  0.6 1.8 %pack.1 = bf16[8,24,1664]{2,1,0:T(8,128)(2,1)S(1)} custom-call(s32[1,2]{1,0:T(1,128)} %table_ref.1, bf16[3,8,8,1536]{3,2,1,0:T(8,128)(2,1)} %bitcast.14), custom_call_target="tpu_custom_call" | custom-call | tf_op jit(solution)/shard_map/pack/pallas_call | solution.py:438
  2.4 24.5 %all_to_all.15 = bf16[8,24,1664]{2,1,0:T(8,128)(2,1)S(1)} all-to-all(bf16[8,24,1664]{2,1,0:T(8,128)(2,1)S(1)} %pack.1), channel_id=1, replica_groups=mesh['pole'=4,'grid'=8] {'grid'}, dimensions={0} | all-to-all | bytes 1277952 | tf_op jit(solution)/shard_map/all_to_all | solution.py:447
  26.9 1.2 %select.9 = bf16[8,64,512]{2,1,0:T(8,128)(2,1)} custom-call(bf16[192,1664]{1,0:T(8,128)(2,1)S(1)} %bitcast.12), custom_call_target="tpu_custom_call" | custom-call | tf_op jit(solution)/shard_map/select/pallas_call | solution.py:449
  28.2 3.5 %all-to-all-start.1 = ((bf16[8,64,512]{2,1,0:T(8,128)(2,1)}), bf16[8,64,512]{2,1,0:T(8,128)(2,1)S(1)}, u32[]{:S(2)}, u32[]{:S(2)}) async-start(bf16[8,64,512]{2,1,0:T(8,128)(2,1)} %select.9), calls=%async_computation.1 | async-start | bytes 1048576 | tf_op jit(solution)/shard_map/all_to_all | solution.py:459
  33.0 0.0 copy-start.1
  33.7 0.0 copy-done.1
  33.7 0.2 convert_reduce_fusion
  33.9 0.6 multiply_add_fusion
  34.4 1.4 %order.1 = (bf16[512,256]{1,0:T(8,128)(2,1)S(1)}, bf16[256,512]{1,0:T(8,128)(2,1)S(1)}, bf16[256,256]{1,0:T(8,128)(2,1)S(1)}, bf16[256,256]{1,0:T(8,128)(2,1)S(1)}) custom-call(s32[1]{0:T(128)S(6)} %copy.16.counts_ref, s32[1,256]{1,0:T(1,128)} %bitcast.19, bf16[2,256,256]{2,1,0:T(8,128)(2,1)} %bitcast.15, bf16[256,256]{1,0:T(8,128)(2,1)} %bitcast.16, ...), custom_call_target="tpu_custom_call" | custom-call | tf_op jit(solution)/shard_map/order/pallas_call | solution.py:470
  35.9 9.9 %all-to-all-done.1 = bf16[8,64,512]{2,1,0:T(8,128)(2,1)S(1)} async-done(((bf16[8,64,512]{2,1,0:T(8,128)(2,1)}), bf16[8,64,512]{2,1,0:T(8,128)(2,1)S(1)}, u32[]{:S(2)}, u32[]{:S(2)}) %all-to-all-start.1) | async-done | bytes 524320 | tf_op jit(solution)/shard_map/all_to_all | solution.py:459
  45.8 2.5 %encode.1 = s16[32,56,128]{2,1,0:T(8,128)(2,1)} custom-call(s32[1,2]{1,0:T(1,128)} %hpattern_ref.1, f32[1]{0:T(128)S(6)} %copy.14.weight_ref, f32[1]{0:T(128)S(6)} %copy.15.energy_ref, bf16[512,512]{1,0:T(8,128)(2,1)S(1)} %bitcast.13, bf16[512,256]{1,0:T(8,128)(2,1)S(1)} %get-tuple-element.10.lower_ref, bf16[256,512]{1,0:T(8,128)(2,1)S(1)} %get-tuple-element.11.turned_ref, ...), custom_call_target="tpu_custom_call" | custom-call | tf_op jit(solution)/shard_map/encode/pallas_call | solution.py:482
  48.3 3.7 %all-to-all-start.2 = ((s16[32,56,128]{2,1,0:T(8,128)(2,1)}), s16[32,56,128]{2,1,0:T(8,128)(2,1)S(1)}, u32[]{:S(2)}, u32[]{:S(2)}) async-start(s16[32,56,128]{2,1,0:T(8,128)(2,1)} %encode.1), calls=%async_computation.2 | async-start | bytes 917504 | tf_op jit(solution)/shard_map/all_to_all | solution.py:490
  51.9 0.0 copy-start
  52.0 0.7 copy-done
  52.6 0.2 convert_reduce_fusion.1
  52.8 0.6 multiply_add_fusion.1
  53.4 13.4 %all-to-all-done.2.recv_ref = s16[32,56,128]{2,1,0:T(8,128)(2,1)S(1)} async-done(((s16[32,56,128]{2,1,0:T(8,128)(2,1)}), s16[32,56,128]{2,1,0:T(8,128)(2,1)S(1)}, u32[]{:S(2)}, u32[]{:S(2)}) %all-to-all-start.2) | async-done | bytes 458784 | tf_op jit(solution)/shard_map/all_to_all | solution.py:490
  66.8 1.9 %decode.1 = (bf16[192,256]{1,0:T(8,128)(2,1)}, bf16[192,256]{1,0:T(8,128)(2,1)}, f32[1,1]{1,0:T(1,128)}) custom-call(s32[1]{0:T(128)} %bitcast.odd_ref, s32[1,256]{1,0:T(1,128)} %bitcast.18, s16[32,56,128]{2,1,0:T(8,128)(2,1)S(1)} %all-to-all-done.2.recv_ref), custom_call_target="tpu_custom_call" | custom-call | tf_op jit(solution)/shard_map/decode/pallas_call | solution.py:495
  (2 shorter events, 0.0 us)
Async XLA Ops:
  28.2 17.6 %all-to-all-start.1 = ((bf16[8,64,512]{2,1,0:T(8,128)(2,1)}), bf16[8,64,512]{2,1,0:T(8,128)(2,1)S(1)}, u32[]{:S(2)}, u32[]{:S(2)}) async-start(bf16[8,64,512]{2,1,0:T(8,128)(2,1)} %select.9), calls=%async_computation.1 | async-start | bytes 1048576 | tf_op jit(solution)/shard_map/all_to_all | solution.py:459
  33.0 0.7 copy-start.1
  48.3 18.5 %all-to-all-start.2 = ((s16[32,56,128]{2,1,0:T(8,128)(2,1)}), s16[32,56,128]{2,1,0:T(8,128)(2,1)S(1)}, u32[]{:S(2)}, u32[]{:S(2)}) async-start(s16[32,56,128]{2,1,0:T(8,128)(2,1)} %encode.1), calls=%async_computation.2 | async-start | bytes 917504 | tf_op jit(solution)/shard_map/all_to_all | solution.py:490
  51.9 0.7 copy-start

commit v5 on v4

--- a/solution.py
+++ b/solution.py
@@ -32,7 +32,7 @@
     return pl.BlockSpec(memory_space=SMEM)
 
 
-def pack_kernel(table_ref, rows_ref, out_ref, sems):
+def pack_kernel(table_hbm, rows_ref, out_ref, table_ref, sems):
     stretches, _, _, width = rows_ref.shape
     copies = [
         pltpu.make_async_copy(
@@ -42,6 +42,7 @@
     ]
     for copy in copies:
         copy.start()
+    pltpu.sync_copy(table_hbm, table_ref)
     shares, rows, lanes = out_ref.shape
     lane = lax.broadcasted_iota(jnp.int32, (rows, lanes - width), 1)
     table = jnp.zeros((rows, lanes - width), jnp.float32)
@@ -194,10 +195,25 @@
 
 
 def order_kernel(
-    counts_ref, slot_ref, factor_ref, diag_ref, inter_ref, lower_ref, turned_ref, diag_out, inter_out
+    counts_ref,
+    hpattern_ref,
+    weight_ref,
+    energy_ref,
+    odd_ref,
+    send_ref,
+    recv_ref,
+    factor_ref,
+    diag_ref,
+    inter_ref,
+    lower_ref,
+    turned_ref,
+    diag_out,
+    inter_out,
+    info_ref,
+    slots_ref,
 ):
     blk_count, width, _ = factor_ref.shape
-    one_hot = (lax.broadcasted_iota(jnp.int32, (width, width), 0) == slot_ref[...]).astype(
+    one_hot = (lax.broadcasted_iota(jnp.int32, (width, width), 0) == send_ref[...]).astype(
         jnp.bfloat16
     )
 
@@ -213,6 +229,22 @@
         turned_ref[:, m * width : (m + 1) * width] = turn(block)
     diag_out[...] = turn(diag_ref[...])
     inter_out[...] = turn(inter_ref[...])
+
+    rows, lanes = info_ref.shape
+    row_id = lax.broadcasted_iota(jnp.int32, (rows, lanes), 0)
+    block = lax.broadcasted_iota(jnp.int32, (rows, lanes), 1) // width
+    info = jnp.ones((rows, lanes), jnp.float32)
+    for m in range(blk_count):
+        info = jnp.where(block == m + 1, hpattern_ref[0, m].astype(jnp.float32), info)
+    info = jnp.where(row_id == 1, weight_ref[0], info)
+    for at, scalar in ((2, weight_ref[0]), (4, energy_ref[0])):
+        grown = jnp.full((rows, lanes), scalar) * 2.0**13
+        grown_high = jnp.floor(grown)
+        info = jnp.where(row_id == at, grown_high, info)
+        info = jnp.where(row_id == at + 1, (grown - grown_high) * 2.0**15, info)
+    info_ref[...] = info
+    row_id = lax.broadcasted_iota(jnp.int32, (SUB, width), 0)
+    slots_ref[...] = jnp.where(row_id == 0, recv_ref[...], odd_ref[0])
 
 
 def halved_sum(values):
@@ -241,19 +273,17 @@
 def encode_kernel(
     shares,
     chunk,
-    hpattern_ref,
-    weight_ref,
-    energy_ref,
     rows_ref,
     lower_ref,
     turned_ref,
     diag_ref,
     inter_ref,
+    info_ref,
     out_ref,
     sorted_ref,
 ):
-    blk_count = hpattern_ref.shape[1]
-    width = lower_ref.shape[1]
+    depth, width = lower_ref.shape
+    blk_count = depth // width
     per_blk = width // shares
     for m in range(blk_count):
         for j in range(shares):
@@ -278,19 +308,15 @@
         + jnp.dot(mid, lower, preferred_element_type=jnp.float32)
         + jnp.dot(high, lower, preferred_element_type=jnp.float32)
     )
-    count = weight_ref[0] * halved_sum(diag * inter_ref[...].astype(jnp.float32))
-    parts = [diag] + [
-        off[:, m * width : (m + 1) * width] * hpattern_ref[0, m].astype(jnp.float32)
-        for m in range(blk_count)
-    ]
-    values = jnp.concatenate(parts, axis=1)
+    count = halved_sum(diag * inter_ref[...].astype(jnp.float32))
+    values = jnp.concatenate([diag, off * info_ref[:1, width:]], axis=1)
     largest = jnp.max(jnp.abs(values), axis=0, keepdims=True)
     level = jnp.ceil(jnp.log2(jnp.maximum(largest, TINY)) * FINE)
     codes = jnp.floor(values * (jnp.exp2(level * (-1.0 / FINE)) * STEPS) + 0.5)
 
     row_id = lax.broadcasted_iota(jnp.int32, (SUB, LANES), 0)
     lane_id = lax.broadcasted_iota(jnp.int32, (SUB, LANES), 1)
-    full_count = jnp.full((SUB, LANES), count)
+    full_count = info_ref[1:2, :LANES] * jnp.full((SUB, LANES), count)
     power = jnp.ceil(jnp.log2(jnp.maximum(jnp.abs(full_count), TINY)))
     scaled = full_count * jnp.exp2(-power) * 2.0**14
     scaled_high = jnp.floor(scaled)
@@ -299,11 +325,7 @@
         power,
         jnp.where(lane_id == 1, scaled_high, jnp.floor((scaled - scaled_high) * 2.0**15)),
     )
-    for at, scalar in ((2, weight_ref[0]), (4, energy_ref[0])):
-        grown = jnp.full((SUB, LANES), scalar) * 2.0**13
-        grown_high = jnp.floor(grown)
-        extra = jnp.where(row_id == at, grown_high, extra)
-        extra = jnp.where(row_id == at + 1, (grown - grown_high) * 2.0**15, extra)
+    extra = jnp.where(row_id < 6, info_ref[:, :LANES], extra)
 
     dests, _, _ = out_ref.shape
     pole_count = values.shape[1] // chunk
@@ -335,12 +357,12 @@
 
 
 def decode_kernel(
-    owners, cap, odd_ref, slot_ref, recv_ref, dens_ref, energy_ref, count_ref, full_ref, half_ref
+    owners, cap, slots_ref, recv_ref, dens_ref, energy_ref, count_ref, full_ref, half_ref
 ):
     dests, rows, _ = recv_ref.shape
     poles = dests // owners
     half = cap // 2
-    width = slot_ref.shape[1]
+    width = slots_ref.shape[1]
     count = jnp.zeros((1, 1), jnp.float32)
     lost = jnp.zeros((1, 1), jnp.float32)
     for g in range(owners):
@@ -369,7 +391,7 @@
         half_ref[g * half : (g + 1) * half, LANES:] = sums[3].astype(jnp.bfloat16)
     count_ref[0, 0] = jnp.sum(count + lost)
 
-    slot = slot_ref[...]
+    slot = slots_ref[:1, :]
     pick = (lax.broadcasted_iota(jnp.int32, (owners * cap, width), 0) == slot).astype(jnp.bfloat16)
     row = lax.broadcasted_iota(jnp.int32, (owners * half, width), 0)
     owner = slot // cap
@@ -383,16 +405,17 @@
             held, chosen, (((0,), (0,)), ((), ())), preferred_element_type=jnp.float32
         )
 
-    full = take(full_ref[...], pick).astype(jnp.bfloat16)
+    full = take(full_ref[...], pick)
     by_left = take(half_ref[...], left)
     by_right = take(half_ref[...], right)
     mid = LANES // 2
-    full_at = pl.multiple_of(odd_ref[0] * mid, mid)
-    half_at = pl.multiple_of((1 - odd_ref[0]) * LANES, mid)
+    odd = jnp.broadcast_to(slots_ref[1:2, :], (LANES + mid, width)) == 1
     for at, ref in ((0, dens_ref), (LANES, energy_ref)):
-        ref[pl.ds(full_at, LANES), :] = full[at : at + LANES]
-        joined = by_left[at : at + mid] + by_right[at + mid : at + LANES]
-        ref[pl.ds(half_at, mid), :] = joined.astype(jnp.bfloat16)
+        wide = full[at : at + LANES]
+        slim = by_left[at : at + mid] + by_right[at + mid : at + LANES]
+        ref[...] = jnp.where(
+            odd, jnp.concatenate([slim, wide], axis=0), jnp.concatenate([wide, slim], axis=0)
+        ).astype(jnp.bfloat16)
 
 
 def ranks(own, order):
@@ -440,8 +463,11 @@
             out_shape=VMEM(
                 (grid_count, local_rows // grid_count, anc_rows + LANES), jnp.bfloat16
             ),
-            in_specs=[sspec(), hspec()],
-            scratch_shapes=[pltpu.SemaphoreType.DMA((stretches,))],
+            in_specs=[hspec(), hspec()],
+            scratch_shapes=[
+                SMEM(ancestors.shape, jnp.int32),
+                pltpu.SemaphoreType.DMA((stretches,)),
+            ],
             name="pack",
         )(ancestors, anc_inv[0].reshape(stretches, grid_count, SUB, anc_rows))
         held = lax.all_to_all(sent, "grid", split_axis=0, concat_axis=0, tiled=True)
@@ -465,44 +491,54 @@
     sub_block = sub_block.reshape(blk_count * width, blk_count * width)
 
     if direct:
-        factor, diag, inter = factor_cols[0, 0], diag_inv[0, 0], intersection[0]
-        square = jax.ShapeDtypeStruct((width, width), jnp.bfloat16)
-        lower, turned, diag, inter = pl.pallas_call(
+        odd = (lax.axis_index("pole") & 1).astype(jnp.int32)[None]
+        lower, turned, diag, inter, info, pickup_slots = pl.pallas_call(
             order_kernel,
             out_shape=(
                 VMEM((blk_count * width, width), jnp.bfloat16),
                 VMEM((width, blk_count * width), jnp.bfloat16),
                 VMEM((width, width), jnp.bfloat16),
                 VMEM((width, width), jnp.bfloat16),
+                VMEM((SUB, (blk_count + 1) * width), jnp.float32),
+                VMEM((SUB, width), jnp.int32),
             ),
-            in_specs=[sspec()] + [vspec()] * 4,
+            in_specs=[sspec()] * 5 + [vspec()] * 5,
             name="order",
-        )(counts, send_slot[None], factor, diag, inter)
+        )(
+            counts,
+            hpattern,
+            pole_w,
+            pole_z,
+            odd,
+            send_slot[None],
+            recv_slot[None],
+            factor_cols[0, 0],
+            diag_inv[0, 0],
+            intersection[0],
+        )
         rows = slot_cap * 3 // 2 + SUB
         coded = pl.pallas_call(
             functools.partial(encode_kernel, shares, chunk),
-            out_shape=jax.ShapeDtypeStruct((pole_count * grid_count, rows, LANES), jnp.int16),
-            in_specs=[sspec()] * 3 + [vspec()] * 5,
-            out_specs=vspec(),
+            out_shape=VMEM((pole_count * grid_count, rows, LANES), jnp.int16),
+            in_specs=[vspec()] * 6,
             scratch_shapes=[VMEM((blk_count * width, blk_count * width), jnp.float32)],
             name="encode",
-        )(hpattern, pole_w, pole_z, invmem(sub_block), *map(invmem, (lower, turned, diag, inter)))
+        )(*map(invmem, (sub_block, lower, turned, diag, inter, info)))
         arrived = lax.all_to_all(
             coded, ("pole", "grid"), split_axis=0, concat_axis=0, tiled=True
         )
-        odd = (lax.axis_index("pole") & 1).astype(jnp.int32)[None]
         half = jax.ShapeDtypeStruct((chunk, width), jnp.bfloat16)
         density, energy, electrons = pl.pallas_call(
             functools.partial(decode_kernel, grid_count, slot_cap),
             out_shape=(half, half, jax.ShapeDtypeStruct((1, 1), jnp.float32)),
-            in_specs=[sspec(), vspec(), vspec()],
+            in_specs=[vspec(), vspec()],
             out_specs=(vspec(), vspec(), sspec()),
             scratch_shapes=[
                 VMEM((width, 2 * LANES), jnp.bfloat16),
                 VMEM((width // 2, 2 * LANES), jnp.bfloat16),
             ],
             name="decode",
-        )(odd, recv_slot[None], invmem(arrived))
+        )(invmem(pickup_slots), invmem(arrived))
         return (density.T, energy.T, electrons[0, 0])
 
     stack = pl.pallas_call(

time: 69.1 us -> 66.1 us (0.957)
  blocking collectives: 24.5 us -> 42.8 us
  waiting for transfers between devices: 23.3 us -> 8.6 us
  starting transfers between devices: 7.15 us -> 3.5 us
  Pallas kernels: 8.83 us -> 6.12 us
    all_to_all x0 -> x1, blocking collectives: none -> 18.3 us  [body(): lax.all_to_all(coded, ('pole', 'grid'), split_axis=0, concat_axis=0, tile...]
    all_to_all x1 -> x0, waiting for transfers between devices: 13.4 us -> none  [body(): lax.all_to_all(coded, ('pole', 'grid'), split_axis=0, concat_axis=0, tile...]
    all_to_all x1 -> x0, starting transfers between devices: 3.65 us -> none  [body(): lax.all_to_all(coded, ('pole', 'grid'), split_axis=0, concat_axis=0, tile...]
    pallas_call x1, Pallas kernels: 2.52 us -> 1.09 us  [body(): pl.pallas_call(functools.partial(encode_kernel, shares, chunk), out_shape...]
    all_to_all x1, waiting for transfers between devices: 9.91 us -> 8.6 us  [body(): lax.all_to_all(chosen, 'grid', split_axis=0, concat_axis=0, tiled=True)]
  transfers between devices with their start and end apart: 2 -> 1, of which waited for: 2 -> 1; matrix products, arithmetic and copies ran while one was open for 2% -> 2% of each run, Pallas kernels for 2% -> 2%
where the time goes in v5:
time: 66.1 us; the launch traced here: 65.7 us
  blocking collectives  42.8 us (65%)
  waiting for transfers between devices  8.6 us (13%)
  Pallas kernels  6.12 us (9%)
  starting transfers between devices  3.5 us (5%)
  between operations  2.64 us (4%)
  other arithmetic  1.56 us (2%)
    all_to_all x1, blocking collectives, body(): held = lax.all_to_all(sent, 'grid', split_axis=0, concat_axis=0, tiled=True)  24.5 us
    all_to_all x1, blocking collectives, body(): lax.all_to_all(coded, ('pole', 'grid'), split_axis=0, concat_axis=0, tile...  18.3 us
    all_to_all x1, waiting for transfers between devices, body(): lax.all_to_all(chosen, 'grid', split_axis=0, concat_axis=0, tiled=True)  8.6 us
    all_to_all x1, starting transfers between devices, body(): lax.all_to_all(chosen, 'grid', split_axis=0, concat_axis=0, tiled=True)  3.5 us
    pallas_call x1, Pallas kernels, body(): pl.pallas_call(order_kernel, out_shape=(VMEM((blk_count * width, width),...  1.43 us
  transfers between devices with their start and end apart: 1, of which 1 were waited for; matrix products, arithmetic and copies ran while one was open for 2% of the time, Pallas kernels for 2%

profile of v5, /device:TPU:0, one launch (start us, length us, event | category | flops | bytes accessed | tf_op | source)
XLA Modules:
  0.0 65.7 jit_solution(9898717500942184710)
XLA Ops:
  0.6 1.1 %pack.1 = bf16[8,24,1664]{2,1,0:T(8,128)(2,1)S(1)} custom-call(s32[1,2]{1,0:T(1,128)} %table_hbm.1, bf16[3,8,8,1536]{3,2,1,0:T(8,128)(2,1)} %bitcast.14), custom_call_target="tpu_custom_call" | custom-call | tf_op jit(solution)/shard_map/pack/pallas_call | solution.py:461
  1.8 24.5 %all_to_all.15 = bf16[8,24,1664]{2,1,0:T(8,128)(2,1)S(1)} all-to-all(bf16[8,24,1664]{2,1,0:T(8,128)(2,1)S(1)} %pack.1), channel_id=1, replica_groups=mesh['pole'=4,'grid'=8] {'grid'}, dimensions={0} | all-to-all | bytes 1277952 | tf_op jit(solution)/shard_map/all_to_all | solution.py:473
  26.3 1.2 %select.9 = bf16[8,64,512]{2,1,0:T(8,128)(2,1)} custom-call(bf16[192,1664]{1,0:T(8,128)(2,1)S(1)} %bitcast.12), custom_call_target="tpu_custom_call" | custom-call | tf_op jit(solution)/shard_map/select/pallas_call | solution.py:475
  27.5 0.0 copy-start.1
  27.5 3.5 %all-to-all-start.1 = ((bf16[8,64,512]{2,1,0:T(8,128)(2,1)}), bf16[8,64,512]{2,1,0:T(8,128)(2,1)S(1)}, u32[]{:S(2)}, u32[]{:S(2)}) async-start(bf16[8,64,512]{2,1,0:T(8,128)(2,1)} %select.9), calls=%async_computation.1 | async-start | bytes 1048576 | tf_op jit(solution)/shard_map/all_to_all | solution.py:485
  31.0 0.0 copy-done.1
  33.0 0.0 copy-start
  33.0 0.2 convert_reduce_fusion.1
  33.2 0.5 copy-done
  33.7 0.2 convert_reduce_fusion
  33.9 0.6 multiply_add_fusion.1
  34.5 0.6 multiply_add_fusion
  35.1 1.4 %order.1 = (bf16[512,256]{1,0:T(8,128)(2,1)S(1)}, bf16[256,512]{1,0:T(8,128)(2,1)S(1)}, bf16[256,256]{1,0:T(8,128)(2,1)S(1)}, bf16[256,256]{1,0:T(8,128)(2,1)S(1...) custom-call(s32[1]{0:T(128)S(6)} %copy.16.counts_ref, s32[1,2]{1,0:T(1,128)} %hpattern_ref.1, f32[1]{0:T(128)S(6)} %copy.14.weight_ref, ...), custom_call_target="tpu_custom_call" | custom-call | tf_op jit(solution)/shard_map/order/pallas_call | solution.py:495
  36.5 8.6 %all-to-all-done.1 = bf16[8,64,512]{2,1,0:T(8,128)(2,1)S(1)} async-done(((bf16[8,64,512]{2,1,0:T(8,128)(2,1)}), bf16[8,64,512]{2,1,0:T(8,128)(2,1)S(1)}, u32[]{:S(2)}, u32[]{:S(2)}) %all-to-all-start.1) | async-done | bytes 524320 | tf_op jit(solution)/shard_map/all_to_all | solution.py:485
  45.1 1.1 %encode.1 = s16[32,56,128]{2,1,0:T(8,128)(2,1)S(1)} custom-call(bf16[512,512]{1,0:T(8,128)(2,1)S(1)} %bitcast.13, bf16[512,256]{1,0:T(8,128)(2,1)S(1)} %get-tuple-element.13.lower_ref, bf16[256,512]{1,0:T(8,128)(2,1)S(1)} %get-tuple-element.14.turned_ref, bf16[256,256]{1,0:T(8,128)(2,1)S(1)} %get-tuple-element.15.diag_ref, ...), custom_call_target="tpu_custom_call" | custom-call | tf_op jit(solution)/shard_map/encode/pallas_call | solution.py:520
  46.2 18.3 %all_to_all.16.recv_ref = s16[32,56,128]{2,1,0:T(8,128)(2,1)S(1)} all-to-all(s16[32,56,128]{2,1,0:T(8,128)(2,1)S(1)} %encode.1), channel_id=1, replica_groups=mesh['pole'=4,'grid'=8] {'pole','grid'}, dimensions={0} | all-to-all | bytes 917504 | tf_op jit(solution)/shard_map/all_to_all | solution.py:527
  64.5 1.2 %decode.1 = (bf16[192,256]{1,0:T(8,128)(2,1)}, bf16[192,256]{1,0:T(8,128)(2,1)}, f32[1,1]{1,0:T(1,128)}) custom-call(s32[8,256]{1,0:T(8,128)S(1)} %get-tuple-element.12.slots_ref, s16[32,56,128]{2,1,0:T(8,128)(2,1)S(1)} %all_to_all.16.recv_ref), custom_call_target="tpu_custom_call" | custom-call | tf_op jit(solution)/shard_map/decode/pallas_call | solution.py:531
  (2 shorter events, 0.0 us)
Async XLA Ops:
  27.5 3.5 %copy-start.1 = (s32[256]{0:T(256)S(1)}, s32[256]{0:T(256)}, u32[]{:S(2)}) copy-start(s32[256]{0:T(256)} %param.20) | copy-start | bytes 3076
  27.5 17.6 %all-to-all-start.1 = ((bf16[8,64,512]{2,1,0:T(8,128)(2,1)}), bf16[8,64,512]{2,1,0:T(8,128)(2,1)S(1)}, u32[]{:S(2)}, u32[]{:S(2)}) async-start(bf16[8,64,512]{2,1,0:T(8,128)(2,1)} %select.9), calls=%async_computation.1 | async-start | bytes 1048576 | tf_op jit(solution)/shard_map/all_to_all | solution.py:485
  33.0 0.7 %copy-start = (s32[256]{0:T(256)S(1)}, s32[256]{0:T(256)}, u32[]{:S(2)}) copy-start(s32[256]{0:T(256)} %param.21) | copy-start | bytes 3076

commit v6 on v5

--- a/solution.py
+++ b/solution.py
@@ -55,15 +55,15 @@
         copy.wait()
 
 
-def select_kernel(width, blk_count, held_ref, out_ref, sems):
+def select_kernel(width, blk_count, ring, held_ref, out_ref, sems):
     dests, picked, _ = out_ref.shape
     rows = picked // blk_count
     local = held_ref.shape[0] // dests
     tail = held_ref.shape[1] - LANES
     lane = lax.broadcasted_iota(jnp.int32, (1, LANES), 1)
     copies = []
-    for dest in range(dests):
-        entry = held_ref[dest * local : (dest + 1) * local, tail:].astype(jnp.float32)[:1]
+    for dest, owner in enumerate(ring):
+        entry = held_ref[owner * local : (owner + 1) * local, tail:].astype(jnp.float32)[:1]
         table = [
             jnp.sum(jnp.where(lane == m, entry, 0.0)).astype(jnp.int32) for m in range(blk_count)
         ]
@@ -83,7 +83,7 @@
 
 
 def columns_kernel(
-    shares,
+    ring,
     chunk,
     counts_ref,
     hpattern_ref,
@@ -103,12 +103,13 @@
     ]
     lower = jnp.concatenate(parts, axis=0)
     product = jnp.dot(rows_ref[...], lower, preferred_element_type=jnp.float32)
+    shares = len(ring)
     per_blk = width // shares
     for m in range(blk_count):
         scale = hpattern_ref[0, m].astype(jnp.float32)
-        for j in range(shares):
+        for at_share, j in enumerate(ring):
             for c in range(per_blk // SUB):
-                at = (j * blk_count + m) * per_blk + c * SUB
+                at = (at_share * blk_count + m) * per_blk + c * SUB
                 piece = -product[at : at + SUB]
                 row = m * width + (c * shares + j) * SUB
                 off_ref[row : row + SUB, :] = piece
@@ -271,7 +272,7 @@
 
 
 def encode_kernel(
-    shares,
+    ring,
     chunk,
     rows_ref,
     lower_ref,
@@ -284,10 +285,11 @@
 ):
     depth, width = lower_ref.shape
     blk_count = depth // width
+    shares = len(ring)
     per_blk = width // shares
     for m in range(blk_count):
-        for j in range(shares):
-            at = (j * blk_count + m) * per_blk
+        for place, j in enumerate(ring):
+            at = (place * blk_count + m) * per_blk
             piece = rows_ref[at : at + per_blk, :].astype(jnp.float32)
             for c in range(per_blk // SUB):
                 row = m * width + (c * shares + j) * SUB
@@ -418,6 +420,10 @@
         ).astype(jnp.bfloat16)
 
 
+def ring_order(count):
+    return list(range(0, count, 2)) + list(range(1, count, 2))[::-1]
+
+
 def ranks(own, order):
     same = own[:, None] == own[None, :]
     earlier = order[None, :] < order[:, None]
@@ -456,7 +462,7 @@
 
     spread = grid_count * SUB
     if local_rows % spread == 0 and width % spread == 0:
-        shares = grid_count
+        ring = ring_order(grid_count)
         stretches = local_rows // spread
         sent = pl.pallas_call(
             pack_kernel,
@@ -473,7 +479,7 @@
         held = lax.all_to_all(sent, "grid", split_axis=0, concat_axis=0, tiled=True)
         rows = width // grid_count
         chosen = pl.pallas_call(
-            functools.partial(select_kernel, width, blk_count),
+            functools.partial(select_kernel, width, blk_count, ring),
             out_shape=jax.ShapeDtypeStruct(
                 (grid_count, blk_count * rows, blk_count * width), jnp.bfloat16
             ),
@@ -482,9 +488,11 @@
             scratch_shapes=[pltpu.SemaphoreType.DMA((grid_count, blk_count, blk_count))],
             name="select",
         )(invmem(held.reshape(local_rows, anc_rows + LANES)))
-        sub_block = lax.all_to_all(chosen, "grid", split_axis=0, concat_axis=0, tiled=True)
+        sub_block = lax.all_to_all(
+            chosen, "grid", split_axis=0, concat_axis=0, axis_index_groups=[ring], tiled=True
+        )
     else:
-        shares = 1
+        ring = [0]
         gathered = lax.all_gather(anc_inv[0], "grid", axis=0, tiled=True)
         blocks = gathered.reshape(anc_rows // width, width, anc_rows // width, width)
         sub_block = jnp.take(jnp.take(blocks, ancestors[0], axis=0), ancestors[0], axis=2)
@@ -518,7 +526,7 @@
         )
         rows = slot_cap * 3 // 2 + SUB
         coded = pl.pallas_call(
-            functools.partial(encode_kernel, shares, chunk),
+            functools.partial(encode_kernel, ring, chunk),
             out_shape=VMEM((pole_count * grid_count, rows, LANES), jnp.int16),
             in_specs=[vspec()] * 6,
             scratch_shapes=[VMEM((blk_count * width, blk_count * width), jnp.float32)],
@@ -542,7 +550,7 @@
         return (density.T, energy.T, electrons[0, 0])
 
     stack = pl.pallas_call(
-        functools.partial(columns_kernel, shares, chunk),
+        functools.partial(columns_kernel, ring, chunk),
         out_shape=jax.ShapeDtypeStruct((pole_count, chunk + SUB, width), jnp.float32),
         in_specs=[sspec()] * 4 + [vspec()] * 4,
         out_specs=vspec(),

time: 66.1 us -> 65.3 us (0.988)
  waiting for transfers between devices: 8.6 us -> 7.74 us
    all_to_all x1, waiting for transfers between devices: 8.6 us -> 7.74 us  [body(): lax.all_to_all(chosen, 'grid', split_axis=0, concat_axis=0, axis_index_gr...]
where the time goes in v6:
time: 65.3 us; the launch traced here: 65 us
  blocking collectives  42.9 us (66%)
  waiting for transfers between devices  7.74 us (12%)
  Pallas kernels  6.12 us (9%)
  starting transfers between devices  3.5 us (5%)
  between operations  2.64 us (4%)
  other arithmetic  1.56 us (2%)
    all_to_all x1, blocking collectives, body(): held = lax.all_to_all(sent, 'grid', split_axis=0, concat_axis=0, tiled=True)  24.5 us
    all_to_all x1, blocking collectives, body(): lax.all_to_all(coded, ('pole', 'grid'), split_axis=0, concat_axis=0, tile...  18.4 us
    all_to_all x1, waiting for transfers between devices, body(): lax.all_to_all(chosen, 'grid', split_axis=0, concat_axis=0, axis_index_gr...  7.74 us
    all_to_all x1, starting transfers between devices, body(): lax.all_to_all(chosen, 'grid', split_axis=0, concat_axis=0, axis_index_gr...  3.5 us
    pallas_call x1, Pallas kernels, body(): pl.pallas_call(order_kernel, out_shape=(VMEM((blk_count * width, width),...  1.43 us
  transfers between devices with their start and end apart: 1, of which 1 were waited for; matrix products, arithmetic and copies ran while one was open for 2% of the time, Pallas kernels for 2%

profile of v6, /device:TPU:0, one launch (start us, length us, event | category | flops | bytes accessed | tf_op | source)
XLA Modules:
  0.0 65.0 jit_solution(8966083977622221861)
XLA Ops:
  0.6 1.1 %pack.1 = bf16[8,24,1664]{2,1,0:T(8,128)(2,1)S(1)} custom-call(s32[1,2]{1,0:T(1,128)} %table_hbm.1, bf16[3,8,8,1536]{3,2,1,0:T(8,128)(2,1)} %bitcast.14), custom_call_target="tpu_custom_call" | custom-call | tf_op jit(solution)/shard_map/pack/pallas_call | solution.py:467
  1.8 24.5 %all_to_all.15 = bf16[8,24,1664]{2,1,0:T(8,128)(2,1)S(1)} all-to-all(bf16[8,24,1664]{2,1,0:T(8,128)(2,1)S(1)} %pack.1), channel_id=1, replica_groups=mesh['pole'=4,'grid'=8] {'grid'}, dimensions={0} | all-to-all | bytes 1277952 | tf_op jit(solution)/shard_map/all_to_all | solution.py:479
  26.3 1.2 %select.9 = bf16[8,64,512]{2,1,0:T(8,128)(2,1)} custom-call(bf16[192,1664]{1,0:T(8,128)(2,1)S(1)} %bitcast.12), custom_call_target="tpu_custom_call" | custom-call | tf_op jit(solution)/shard_map/select/pallas_call | solution.py:481
  27.5 0.0 copy-start.1
  27.5 3.5 %all-to-all-start.1 = ((bf16[8,64,512]{2,1,0:T(8,128)(2,1)}), bf16[8,64,512]{2,1,0:T(8,128)(2,1)S(1)}, u32[]{:S(2)}, u32[]{:S(2)}) async-start(bf16[8,64,512]{2,1,0:T(8,128)(2,1)} %select.9), calls=%async_computation.1 | async-start | bytes 1048576 | tf_op jit(solution)/shard_map/all_to_all | solution.py:491
  31.0 0.0 copy-done.1
  33.0 0.0 copy-start
  33.0 0.2 convert_reduce_fusion.1
  33.2 0.5 copy-done
  33.7 0.2 convert_reduce_fusion
  33.9 0.6 multiply_add_fusion.1
  34.5 0.6 multiply_add_fusion
  35.1 1.4 %order.1 = (bf16[512,256]{1,0:T(8,128)(2,1)S(1)}, bf16[256,512]{1,0:T(8,128)(2,1)S(1)}, bf16[256,256]{1,0:T(8,128)(2,1)S(1)}, bf16[256,256]{1,0:T(8,128)(2,1)S(1...) custom-call(s32[1]{0:T(128)S(6)} %copy.16.counts_ref, s32[1,2]{1,0:T(1,128)} %hpattern_ref.1, f32[1]{0:T(128)S(6)} %copy.14.weight_ref, ...), custom_call_target="tpu_custom_call" | custom-call | tf_op jit(solution)/shard_map/order/pallas_call | solution.py:503
  36.5 7.7 %all-to-all-done.1 = bf16[8,64,512]{2,1,0:T(8,128)(2,1)S(1)} async-done(((bf16[8,64,512]{2,1,0:T(8,128)(2,1)}), bf16[8,64,512]{2,1,0:T(8,128)(2,1)S(1)}, u32[]{:S(2)}, u32[]{:S(2)}) %all-to-all-start.1) | async-done | bytes 524320 | tf_op jit(solution)/shard_map/all_to_all | solution.py:491
  44.2 1.1 %encode.1 = s16[32,56,128]{2,1,0:T(8,128)(2,1)S(1)} custom-call(bf16[512,512]{1,0:T(8,128)(2,1)S(1)} %bitcast.13, bf16[512,256]{1,0:T(8,128)(2,1)S(1)} %get-tuple-element.13.lower_ref, bf16[256,512]{1,0:T(8,128)(2,1)S(1)} %get-tuple-element.14.turned_ref, bf16[256,256]{1,0:T(8,128)(2,1)S(1)} %get-tuple-element.15.diag_ref, ...), custom_call_target="tpu_custom_call" | custom-call | tf_op jit(solution)/shard_map/encode/pallas_call | solution.py:528
  45.3 18.4 %all_to_all.16.recv_ref = s16[32,56,128]{2,1,0:T(8,128)(2,1)S(1)} all-to-all(s16[32,56,128]{2,1,0:T(8,128)(2,1)S(1)} %encode.1), channel_id=1, replica_groups=mesh['pole'=4,'grid'=8] {'pole','grid'}, dimensions={0} | all-to-all | bytes 917504 | tf_op jit(solution)/shard_map/all_to_all | solution.py:535
  63.7 1.2 %decode.1 = (bf16[192,256]{1,0:T(8,128)(2,1)}, bf16[192,256]{1,0:T(8,128)(2,1)}, f32[1,1]{1,0:T(1,128)}) custom-call(s32[8,256]{1,0:T(8,128)S(1)} %get-tuple-element.12.slots_ref, s16[32,56,128]{2,1,0:T(8,128)(2,1)S(1)} %all_to_all.16.recv_ref), custom_call_target="tpu_custom_call" | custom-call | tf_op jit(solution)/shard_map/decode/pallas_call | solution.py:539
  (2 shorter events, 0.0 us)
Async XLA Ops:
  27.5 3.5 %copy-start.1 = (s32[256]{0:T(256)S(1)}, s32[256]{0:T(256)}, u32[]{:S(2)}) copy-start(s32[256]{0:T(256)} %param.20) | copy-start | bytes 3076
  27.5 16.7 %all-to-all-start.1 = ((bf16[8,64,512]{2,1,0:T(8,128)(2,1)}), bf16[8,64,512]{2,1,0:T(8,128)(2,1)S(1)}, u32[]{:S(2)}, u32[]{:S(2)}) async-start(bf16[8,64,512]{2,1,0:T(8,128)(2,1)} %select.9), calls=%async_computation.1 | async-start | bytes 1048576 | tf_op jit(solution)/shard_map/all_to_all | solution.py:491
  33.0 0.7 %copy-start = (s32[256]{0:T(256)S(1)}, s32[256]{0:T(256)}, u32[]{:S(2)}) copy-start(s32[256]{0:T(256)} %param.21) | copy-start | bytes 3076

commit v7 on v5

--- a/solution.py
+++ b/solution.py
@@ -33,53 +33,56 @@
 
 
 def pack_kernel(table_hbm, rows_ref, out_ref, table_ref, sems):
-    stretches, _, _, width = rows_ref.shape
+    stretches, shares, rows, width = rows_ref.shape
     copies = [
         pltpu.make_async_copy(
-            rows_ref.at[c], out_ref.at[:, c * SUB : (c + 1) * SUB, :width], sems.at[c]
+            rows_ref.at[c], out_ref.at[:, :, c * width : (c + 1) * width], sems.at[c]
         )
         for c in range(stretches)
     ]
     for copy in copies:
         copy.start()
     pltpu.sync_copy(table_hbm, table_ref)
-    shares, rows, lanes = out_ref.shape
-    lane = lax.broadcasted_iota(jnp.int32, (rows, lanes - width), 1)
-    table = jnp.zeros((rows, lanes - width), jnp.float32)
+    lane = lax.broadcasted_iota(jnp.int32, (rows, LANES), 1)
+    table = jnp.zeros((rows, LANES), jnp.float32)
     for m in range(table_ref.shape[1]):
         table = jnp.where(lane == m, table_ref[0, m].astype(jnp.float32), table)
     table = table.astype(jnp.bfloat16)
-    for j in range(shares):
-        out_ref[j, :, width:] = table
+    for s in range(shares):
+        out_ref[s, :, stretches * width :] = table
     for copy in copies:
         copy.wait()
 
 
-def select_kernel(width, blk_count, held_ref, out_ref, sems):
+def select_kernel(width, blk_count, stretches, held_ref, out_ref, sem):
     dests, picked, _ = out_ref.shape
-    rows = picked // blk_count
-    local = held_ref.shape[0] // dests
-    tail = held_ref.shape[1] - LANES
+    tail = held_ref.shape[2] - LANES
+    per_blk = picked // blk_count // SUB
     lane = lax.broadcasted_iota(jnp.int32, (1, LANES), 1)
-    copies = []
-    for dest in range(dests):
-        entry = held_ref[dest * local : (dest + 1) * local, tail:].astype(jnp.float32)[:1]
-        table = [
-            jnp.sum(jnp.where(lane == m, entry, 0.0)).astype(jnp.int32) for m in range(blk_count)
-        ]
+    tables = []
+    for s in range(dests):
+        entry = held_ref[s, :, tail:].astype(jnp.float32)[:1]
+        tables.append(
+            [jnp.sum(jnp.where(lane == m, entry, 0.0)).astype(jnp.int32) for m in range(blk_count)]
+        )
+    long = tail // stretches
+    for s, table in enumerate(tables):
         for m in range(blk_count):
-            row_at = pl.multiple_of(table[m] * rows, rows)
-            for n in range(blk_count):
-                col_at = pl.multiple_of(table[n] * width, width)
-                copy = pltpu.make_async_copy(
-                    held_ref.at[pl.ds(row_at, rows), pl.ds(col_at, width)],
-                    out_ref.at[dest, m * rows : (m + 1) * rows, n * width : (n + 1) * width],
-                    sems.at[dest, m, n],
-                )
-                copy.start()
-                copies.append(copy)
-    for copy in copies:
-        copy.wait()
+            for k in range(per_blk):
+                stretch = table[m] * per_blk + k
+                device = stretch // stretches
+                start = (stretch - device * stretches) * long
+                back = device // 2
+                place = jnp.where(device == 2 * back, back, dests - 1 - back)
+                at = (m * per_blk + k) * SUB
+                for n in range(blk_count):
+                    col_at = pl.multiple_of(start + table[n] * width, LANES)
+                    pltpu.make_async_copy(
+                        held_ref.at[place, :, pl.ds(col_at, width)],
+                        out_ref.at[s, at : at + SUB, n * width : (n + 1) * width],
+                        sem,
+                    ).start()
+    pltpu.make_async_copy(out_ref, out_ref, sem).wait()
 
 
 def columns_kernel(
@@ -418,6 +421,10 @@
         ).astype(jnp.bfloat16)
 
 
+def ring_order(count):
+    return list(range(0, count, 2)) + list(range(1, count, 2))[::-1]
+
+
 def ranks(own, order):
     same = own[:, None] == own[None, :]
     earlier = order[None, :] < order[:, None]
@@ -456,13 +463,11 @@
 
     spread = grid_count * SUB
     if local_rows % spread == 0 and width % spread == 0:
-        shares = grid_count
+        shares, ring = grid_count, ring_order(grid_count)
         stretches = local_rows // spread
         sent = pl.pallas_call(
             pack_kernel,
-            out_shape=VMEM(
-                (grid_count, local_rows // grid_count, anc_rows + LANES), jnp.bfloat16
-            ),
+            out_shape=VMEM((grid_count, SUB, stretches * anc_rows + LANES), jnp.bfloat16),
             in_specs=[hspec(), hspec()],
             scratch_shapes=[
                 SMEM(ancestors.shape, jnp.int32),
@@ -470,19 +475,23 @@
             ],
             name="pack",
         )(ancestors, anc_inv[0].reshape(stretches, grid_count, SUB, anc_rows))
-        held = lax.all_to_all(sent, "grid", split_axis=0, concat_axis=0, tiled=True)
+        held = lax.all_to_all(
+            sent, "grid", split_axis=0, concat_axis=0, axis_index_groups=[ring], tiled=True
+        )
         rows = width // grid_count
         chosen = pl.pallas_call(
-            functools.partial(select_kernel, width, blk_count),
+            functools.partial(select_kernel, width, blk_count, stretches),
             out_shape=jax.ShapeDtypeStruct(
                 (grid_count, blk_count * rows, blk_count * width), jnp.bfloat16
             ),
             in_specs=[vspec()],
             out_specs=hspec(),
-            scratch_shapes=[pltpu.SemaphoreType.DMA((grid_count, blk_count, blk_count))],
+            scratch_shapes=[pltpu.SemaphoreType.DMA(())],
             name="select",
-        )(invmem(held.reshape(local_rows, anc_rows + LANES)))
-        sub_block = lax.all_to_all(chosen, "grid", split_axis=0, concat_axis=0, tiled=True)
+        )(invmem(held))
+        sub_block = lax.all_to_all(
+            chosen, "grid", split_axis=0, concat_axis=0, axis_index_groups=[ring], tiled=True
+        )
     else:
         shares = 1
         gathered = lax.all_gather(anc_inv[0], "grid", axis=0, tiled=True)

time: 66.1 us -> 64.7 us (0.979)
  waiting for transfers between devices: 8.6 us -> 7.12 us
    all_to_all x1, waiting for transfers between devices: 8.6 us -> 7.12 us  [body(): lax.all_to_all(chosen, 'grid', split_axis=0, concat_axis=0, axis_index_gr...]
where the time goes in v7:
time: 64.7 us; the launch traced here: 64.4 us
  blocking collectives  42.3 us (65%)
  waiting for transfers between devices  7.12 us (11%)
  Pallas kernels  6.71 us (10%)
  starting transfers between devices  3.5 us (5%)
  between operations  2.64 us (4%)
  other arithmetic  1.56 us (2%)
    all_to_all x1, blocking collectives, body(): lax.all_to_all(sent, 'grid', split_axis=0, concat_axis=0, axis_index_grou...  23.9 us
    all_to_all x1, blocking collectives, body(): lax.all_to_all(coded, ('pole', 'grid'), split_axis=0, concat_axis=0, tile...  18.4 us
    all_to_all x1, waiting for transfers between devices, body(): lax.all_to_all(chosen, 'grid', split_axis=0, concat_axis=0, axis_index_gr...  7.12 us
    all_to_all x1, starting transfers between devices, body(): lax.all_to_all(chosen, 'grid', split_axis=0, concat_axis=0, axis_index_gr...  3.5 us
    pallas_call x1, Pallas kernels, body(): pl.pallas_call(functools.partial(select_kernel, width, blk_count, stretch...  1.82 us
    pallas_call x1, Pallas kernels, body(): pl.pallas_call(order_kernel, out_shape=(VMEM((blk_count * width, width),...  1.43 us
  transfers between devices with their start and end apart: 1, of which 1 were waited for; matrix products, arithmetic and copies ran while one was open for 2% of the time, Pallas kernels for 2%

profile of v7, /device:TPU:0, one launch (start us, length us, event | category | flops | bytes accessed | tf_op | source)
XLA Modules:
  0.0 64.4 jit_solution(11935983499473716851)
XLA Ops:
  0.6 1.1 %pack.1 = bf16[8,8,4736]{2,1,0:T(8,128)(2,1)S(1)} custom-call(s32[1,2]{1,0:T(1,128)} %table_hbm.1, bf16[3,8,8,1536]{3,2,1,0:T(8,128)(2,1)} %bitcast.12), custom_call_target="tpu_custom_call" | custom-call | tf_op jit(solution)/shard_map/pack/pallas_call | solution.py:468
  1.8 23.9 %all_to_all.15.held_ref = bf16[8,8,4736]{2,1,0:T(8,128)(2,1)S(1)} all-to-all(bf16[8,8,4736]{2,1,0:T(8,128)(2,1)S(1)} %pack.1), channel_id=1, replica_groups={{0,2,4,6,7,5,3,1},{8,10,12,14,15,13,11,9},{16,18,20,22,23,21,19,17},{24..., dimensions={0} | all-to-all | bytes 1212416 | tf_op jit(solution)/shard_map/all_to_all | solution.py:478
  25.7 1.8 %select.9 = bf16[8,64,512]{2,1,0:T(8,128)(2,1)} custom-call(bf16[8,8,4736]{2,1,0:T(8,128)(2,1)S(1)} %all_to_all.15.held_ref), custom_call_target="tpu_custom_call" | custom-call | tf_op jit(solution)/shard_map/select/pallas_call | solution.py:482
  27.5 0.0 copy-start.1
  27.5 3.5 %all-to-all-start.1 = ((bf16[8,64,512]{2,1,0:T(8,128)(2,1)}), bf16[8,64,512]{2,1,0:T(8,128)(2,1)S(1)}, u32[]{:S(2)}, u32[]{:S(2)}) async-start(bf16[8,64,512]{2,1,0:T(8,128)(2,1)} %select.9), calls=%async_computation.1 | async-start | bytes 1048576 | tf_op jit(solution)/shard_map/all_to_all | solution.py:492
  31.1 0.0 copy-done.1
  33.0 0.0 copy-start
  33.0 0.2 convert_reduce_fusion.1
  33.2 0.5 copy-done
  33.7 0.2 convert_reduce_fusion
  33.9 0.6 multiply_add_fusion.1
  34.5 0.6 multiply_add_fusion
  35.1 1.4 %order.1 = (bf16[512,256]{1,0:T(8,128)(2,1)S(1)}, bf16[256,512]{1,0:T(8,128)(2,1)S(1)}, bf16[256,256]{1,0:T(8,128)(2,1)S(1)}, bf16[256,256]{1,0:T(8,128)(2,1)S(1...) custom-call(s32[1]{0:T(128)S(6)} %copy.16.counts_ref, s32[1,2]{1,0:T(1,128)} %hpattern_ref.1, f32[1]{0:T(128)S(6)} %copy.14.weight_ref, ...), custom_call_target="tpu_custom_call" | custom-call | tf_op jit(solution)/shard_map/order/pallas_call | solution.py:504
  36.5 7.1 %all-to-all-done.1 = bf16[8,64,512]{2,1,0:T(8,128)(2,1)S(1)} async-done(((bf16[8,64,512]{2,1,0:T(8,128)(2,1)}), bf16[8,64,512]{2,1,0:T(8,128)(2,1)S(1)}, u32[]{:S(2)}, u32[]{:S(2)}) %all-to-all-start.1) | async-done | bytes 524320 | tf_op jit(solution)/shard_map/all_to_all | solution.py:492
  43.6 1.1 %encode.1 = s16[32,56,128]{2,1,0:T(8,128)(2,1)S(1)} custom-call(bf16[512,512]{1,0:T(8,128)(2,1)S(1)} %bitcast.11, bf16[512,256]{1,0:T(8,128)(2,1)S(1)} %get-tuple-element.13.lower_ref, bf16[256,512]{1,0:T(8,128)(2,1)S(1)} %get-tuple-element.14.turned_ref, bf16[256,256]{1,0:T(8,128)(2,1)S(1)} %get-tuple-element.15.diag_ref, ...), custom_call_target="tpu_custom_call" | custom-call | tf_op jit(solution)/shard_map/encode/pallas_call | solution.py:529
  44.7 18.4 %all_to_all.16.recv_ref = s16[32,56,128]{2,1,0:T(8,128)(2,1)S(1)} all-to-all(s16[32,56,128]{2,1,0:T(8,128)(2,1)S(1)} %encode.1), channel_id=1, replica_groups=mesh['pole'=4,'grid'=8] {'pole','grid'}, dimensions={0} | all-to-all | bytes 917504 | tf_op jit(solution)/shard_map/all_to_all | solution.py:536
  63.1 1.2 %decode.1 = (bf16[192,256]{1,0:T(8,128)(2,1)}, bf16[192,256]{1,0:T(8,128)(2,1)}, f32[1,1]{1,0:T(1,128)}) custom-call(s32[8,256]{1,0:T(8,128)S(1)} %get-tuple-element.12.slots_ref, s16[32,56,128]{2,1,0:T(8,128)(2,1)S(1)} %all_to_all.16.recv_ref), custom_call_target="tpu_custom_call" | custom-call | tf_op jit(solution)/shard_map/decode/pallas_call | solution.py:540
  (2 shorter events, 0.0 us)
Async XLA Ops:
  27.5 3.5 %copy-start.1 = (s32[256]{0:T(256)S(1)}, s32[256]{0:T(256)}, u32[]{:S(2)}) copy-start(s32[256]{0:T(256)} %param.20) | copy-start | bytes 3076
  27.5 16.1 %all-to-all-start.1 = ((bf16[8,64,512]{2,1,0:T(8,128)(2,1)}), bf16[8,64,512]{2,1,0:T(8,128)(2,1)S(1)}, u32[]{:S(2)}, u32[]{:S(2)}) async-start(bf16[8,64,512]{2,1,0:T(8,128)(2,1)} %select.9), calls=%async_computation.1 | async-start | bytes 1048576 | tf_op jit(solution)/shard_map/all_to_all | solution.py:492
  33.0 0.7 %copy-start = (s32[256]{0:T(256)S(1)}, s32[256]{0:T(256)}, u32[]{:S(2)}) copy-start(s32[256]{0:T(256)} %param.21) | copy-start | bytes 3076

commit v8 on v7

--- a/solution.py
+++ b/solution.py
@@ -276,6 +276,7 @@
 def encode_kernel(
     shares,
     chunk,
+    places,
     rows_ref,
     lower_ref,
     turned_ref,
@@ -351,7 +352,7 @@
         tail = whole(tail)
         for g in range(owners):
             rows = slice(g * cap, (g + 1) * cap)
-            d = q * owners + g
+            d = places[q * owners + g]
             out_ref[d, :cap, :] = whole(codes[rows, full_at : full_at + LANES])
             out_ref[d, cap : cap + half, :] = whole(
                 fold_half(codes[rows, half_at : half_at + LANES], right)
@@ -360,7 +361,7 @@
 
 
 def decode_kernel(
-    owners, cap, slots_ref, recv_ref, dens_ref, energy_ref, count_ref, full_ref, half_ref
+    owners, cap, places, slots_ref, recv_ref, dens_ref, energy_ref, count_ref, full_ref, half_ref
 ):
     dests, rows, _ = recv_ref.shape
     poles = dests // owners
@@ -371,7 +372,7 @@
     for g in range(owners):
         sums = [0.0, 0.0, 0.0, 0.0]
         for p in range(poles):
-            piece = recv_ref[p * owners + g].astype(jnp.int32).astype(jnp.float32)
+            piece = recv_ref[places[p * owners + g]].astype(jnp.int32).astype(jnp.float32)
             extra = piece[cap + half :]
             scale = jnp.exp2(extra[:2] * (1.0 / FINE)) * (1.0 / STEPS)
             weight = extra[2:3] * 2.0**-13 + extra[3:4] * 2.0**-28
@@ -525,20 +526,29 @@
             diag_inv[0, 0],
             intersection[0],
         )
+        everyone = [
+            p * grid_count + g for g in ring_order(grid_count) for p in ring_order(pole_count)
+        ]
+        places = {device: at for at, device in enumerate(everyone)}
         rows = slot_cap * 3 // 2 + SUB
         coded = pl.pallas_call(
-            functools.partial(encode_kernel, shares, chunk),
+            functools.partial(encode_kernel, shares, chunk, places),
             out_shape=VMEM((pole_count * grid_count, rows, LANES), jnp.int16),
             in_specs=[vspec()] * 6,
             scratch_shapes=[VMEM((blk_count * width, blk_count * width), jnp.float32)],
             name="encode",
         )(*map(invmem, (sub_block, lower, turned, diag, inter, info)))
         arrived = lax.all_to_all(
-            coded, ("pole", "grid"), split_axis=0, concat_axis=0, tiled=True
+            coded,
+            ("pole", "grid"),
+            split_axis=0,
+            concat_axis=0,
+            axis_index_groups=[everyone],
+            tiled=True,
         )
         half = jax.ShapeDtypeStruct((chunk, width), jnp.bfloat16)
         density, energy, electrons = pl.pallas_call(
-            functools.partial(decode_kernel, grid_count, slot_cap),
+            functools.partial(decode_kernel, grid_count, slot_cap, places),
             out_shape=(half, half, jax.ShapeDtypeStruct((1, 1), jnp.float32)),
             in_specs=[vspec(), vspec()],
             out_specs=(vspec(), vspec(), sspec()),

time: 64.7 us -> 63.7 us (0.985)
  blocking collectives: 42.3 us -> 41.3 us
    all_to_all x1, blocking collectives: 18.4 us -> 17.4 us  [body(): lax.all_to_all(coded, ('pole', 'grid'), split_axis=0, concat_axis=0, axis...]
where the time goes in v8:
time: 63.7 us; the launch traced here: 63.3 us
  blocking collectives  41.3 us (65%)
  waiting for transfers between devices  7.12 us (11%)
  Pallas kernels  6.7 us (11%)
  starting transfers between devices  3.5 us (5%)
  between operations  2.64 us (4%)
  other arithmetic  1.56 us (2%)
    all_to_all x1, blocking collectives, body(): lax.all_to_all(sent, 'grid', split_axis=0, concat_axis=0, axis_index_grou...  23.9 us
    all_to_all x1, blocking collectives, body(): lax.all_to_all(coded, ('pole', 'grid'), split_axis=0, concat_axis=0, axis...  17.4 us
    all_to_all x1, waiting for transfers between devices, body(): lax.all_to_all(chosen, 'grid', split_axis=0, concat_axis=0, axis_index_gr...  7.12 us
    all_to_all x1, starting transfers between devices, body(): lax.all_to_all(chosen, 'grid', split_axis=0, concat_axis=0, axis_index_gr...  3.5 us
    pallas_call x1, Pallas kernels, body(): pl.pallas_call(functools.partial(select_kernel, width, blk_count, stretch...  1.82 us
    pallas_call x1, Pallas kernels, body(): pl.pallas_call(order_kernel, out_shape=(VMEM((blk_count * width, width),...  1.43 us
  transfers between devices with their start and end apart: 1, of which 1 were waited for; matrix products, arithmetic and copies ran while one was open for 2% of the time, Pallas kernels for 2%

profile of v8, /device:TPU:0, one launch (start us, length us, event | category | flops | bytes accessed | tf_op | source)
XLA Modules:
  0.0 63.3 jit_solution(9693839682627480775)
XLA Ops:
  0.6 1.1 %pack.1 = bf16[8,8,4736]{2,1,0:T(8,128)(2,1)S(1)} custom-call(s32[1,2]{1,0:T(1,128)} %table_hbm.1, bf16[3,8,8,1536]{3,2,1,0:T(8,128)(2,1)} %bitcast.12), custom_call_target="tpu_custom_call" | custom-call | tf_op jit(solution)/shard_map/pack/pallas_call | solution.py:469
  1.8 23.9 %all_to_all.15.held_ref = bf16[8,8,4736]{2,1,0:T(8,128)(2,1)S(1)} all-to-all(bf16[8,8,4736]{2,1,0:T(8,128)(2,1)S(1)} %pack.1), channel_id=1, replica_groups={{0,2,4,6,7,5,3,1},{8,10,12,14,15,13,11,9},{16,18,20,22,23,21,19,17},{24..., dimensions={0} | all-to-all | bytes 1212416 | tf_op jit(solution)/shard_map/all_to_all | solution.py:479
  25.7 1.8 %select.9 = bf16[8,64,512]{2,1,0:T(8,128)(2,1)} custom-call(bf16[8,8,4736]{2,1,0:T(8,128)(2,1)S(1)} %all_to_all.15.held_ref), custom_call_target="tpu_custom_call" | custom-call | tf_op jit(solution)/shard_map/select/pallas_call | solution.py:483
  27.5 0.0 copy-start.1
  27.5 3.5 %all-to-all-start.1 = ((bf16[8,64,512]{2,1,0:T(8,128)(2,1)}), bf16[8,64,512]{2,1,0:T(8,128)(2,1)S(1)}, u32[]{:S(2)}, u32[]{:S(2)}) async-start(bf16[8,64,512]{2,1,0:T(8,128)(2,1)} %select.9), calls=%async_computation.1 | async-start | bytes 1048576 | tf_op jit(solution)/shard_map/all_to_all | solution.py:493
  31.1 0.0 copy-done.1
  33.0 0.0 copy-start
  33.0 0.2 convert_reduce_fusion.1
  33.2 0.5 copy-done
  33.7 0.2 convert_reduce_fusion
  33.9 0.6 multiply_add_fusion.1
  34.5 0.6 multiply_add_fusion
  35.1 1.4 %order.1 = (bf16[512,256]{1,0:T(8,128)(2,1)S(1)}, bf16[256,512]{1,0:T(8,128)(2,1)S(1)}, bf16[256,256]{1,0:T(8,128)(2,1)S(1)}, bf16[256,256]{1,0:T(8,128)(2,1)S(1...) custom-call(s32[1]{0:T(128)S(6)} %copy.16.counts_ref, s32[1,2]{1,0:T(1,128)} %hpattern_ref.1, f32[1]{0:T(128)S(6)} %copy.14.weight_ref, ...), custom_call_target="tpu_custom_call" | custom-call | tf_op jit(solution)/shard_map/order/pallas_call | solution.py:505
  36.5 7.1 %all-to-all-done.1 = bf16[8,64,512]{2,1,0:T(8,128)(2,1)S(1)} async-done(((bf16[8,64,512]{2,1,0:T(8,128)(2,1)}), bf16[8,64,512]{2,1,0:T(8,128)(2,1)S(1)}, u32[]{:S(2)}, u32[]{:S(2)}) %all-to-all-start.1) | async-done | bytes 524320 | tf_op jit(solution)/shard_map/all_to_all | solution.py:493
  43.6 1.1 %encode.1 = s16[32,56,128]{2,1,0:T(8,128)(2,1)S(1)} custom-call(bf16[512,512]{1,0:T(8,128)(2,1)S(1)} %bitcast.11, bf16[512,256]{1,0:T(8,128)(2,1)S(1)} %get-tuple-element.13.lower_ref, bf16[256,512]{1,0:T(8,128)(2,1)S(1)} %get-tuple-element.14.turned_ref, bf16[256,256]{1,0:T(8,128)(2,1)S(1)} %get-tuple-element.15.diag_ref, ...), custom_call_target="tpu_custom_call" | custom-call | tf_op jit(solution)/shard_map/encode/pallas_call | solution.py:534
  44.7 17.4 %all_to_all.16.recv_ref = s16[32,56,128]{2,1,0:T(8,128)(2,1)S(1)} all-to-all(s16[32,56,128]{2,1,0:T(8,128)(2,1)S(1)} %encode.1), channel_id=1, replica_groups={{0,16,24,8,2,18,26,10,4,20,28,12,6,22,30,14,7,23,31,15,5,21,29,13,3,19,..., dimensions={0} | all-to-all | bytes 917504 | tf_op jit(solution)/shard_map/all_to_all | solution.py:541
  62.1 1.2 %decode.1 = (bf16[192,256]{1,0:T(8,128)(2,1)}, bf16[192,256]{1,0:T(8,128)(2,1)}, f32[1,1]{1,0:T(1,128)}) custom-call(s32[8,256]{1,0:T(8,128)S(1)} %get-tuple-element.12.slots_ref, s16[32,56,128]{2,1,0:T(8,128)(2,1)S(1)} %all_to_all.16.recv_ref), custom_call_target="tpu_custom_call" | custom-call | tf_op jit(solution)/shard_map/decode/pallas_call | solution.py:550
  (2 shorter events, 0.0 us)
Async XLA Ops:
  27.5 3.5 %copy-start.1 = (s32[256]{0:T(256)S(1)}, s32[256]{0:T(256)}, u32[]{:S(2)}) copy-start(s32[256]{0:T(256)} %param.20) | copy-start | bytes 3076
  27.5 16.1 %all-to-all-start.1 = ((bf16[8,64,512]{2,1,0:T(8,128)(2,1)}), bf16[8,64,512]{2,1,0:T(8,128)(2,1)S(1)}, u32[]{:S(2)}, u32[]{:S(2)}) async-start(bf16[8,64,512]{2,1,0:T(8,128)(2,1)} %select.9), calls=%async_computation.1 | async-start | bytes 1048576 | tf_op jit(solution)/shard_map/all_to_all | solution.py:493
  33.0 0.7 %copy-start = (s32[256]{0:T(256)S(1)}, s32[256]{0:T(256)}, u32[]{:S(2)}) copy-start(s32[256]{0:T(256)} %param.21) | copy-start | bytes 3076

commit v9 on v8

--- a/solution.py
+++ b/solution.py
@@ -58,13 +58,10 @@
     dests, picked, _ = out_ref.shape
     tail = held_ref.shape[2] - LANES
     per_blk = picked // blk_count // SUB
-    lane = lax.broadcasted_iota(jnp.int32, (1, LANES), 1)
     tables = []
     for s in range(dests):
-        entry = held_ref[s, :, tail:].astype(jnp.float32)[:1]
-        tables.append(
-            [jnp.sum(jnp.where(lane == m, entry, 0.0)).astype(jnp.int32) for m in range(blk_count)]
-        )
+        entry = held_ref[s, :, tail:].astype(jnp.float32)
+        tables.append([entry[0, m].astype(jnp.int32) for m in range(blk_count)])
     long = tail // stretches
     for s, table in enumerate(tables):
         for m in range(blk_count):

time: 63.7 us -> 63.6 us (level)
  no operation moved by 1% of the time
where the time goes in v9:
time: 63.6 us; the launch traced here: 63.3 us
  blocking collectives  41.3 us (65%)
  waiting for transfers between devices  7.12 us (11%)
  Pallas kernels  6.66 us (10%)
  starting transfers between devices  3.5 us (6%)
  between operations  2.64 us (4%)
  other arithmetic  1.56 us (2%)
    all_to_all x1, blocking collectives, body(): lax.all_to_all(sent, 'grid', split_axis=0, concat_axis=0, axis_index_grou...  23.9 us
    all_to_all x1, blocking collectives, body(): lax.all_to_all(coded, ('pole', 'grid'), split_axis=0, concat_axis=0, axis...  17.4 us
    all_to_all x1, waiting for transfers between devices, body(): lax.all_to_all(chosen, 'grid', split_axis=0, concat_axis=0, axis_index_gr...  7.12 us
    all_to_all x1, starting transfers between devices, body(): lax.all_to_all(chosen, 'grid', split_axis=0, concat_axis=0, axis_index_gr...  3.5 us
    pallas_call x1, Pallas kernels, body(): pl.pallas_call(functools.partial(select_kernel, width, blk_count, stretch...  1.78 us
    pallas_call x1, Pallas kernels, body(): pl.pallas_call(order_kernel, out_shape=(VMEM((blk_count * width, width),...  1.43 us
  transfers between devices with their start and end apart: 1, of which 1 were waited for; matrix products, arithmetic and copies ran while one was open for 2% of the time, Pallas kernels for 2%

profile of v9, /device:TPU:0, one launch (start us, length us, event | category | flops | bytes accessed | tf_op | source)
XLA Modules:
  0.0 63.3 jit_solution(4051232218039401609)
XLA Ops:
  0.6 1.1 %pack.1 = bf16[8,8,4736]{2,1,0:T(8,128)(2,1)S(1)} custom-call(s32[1,2]{1,0:T(1,128)} %table_hbm.1, bf16[3,8,8,1536]{3,2,1,0:T(8,128)(2,1)} %bitcast.12), custom_call_target="tpu_custom_call" | custom-call | tf_op jit(solution)/shard_map/pack/pallas_call | solution.py:466
  1.8 23.9 %all_to_all.15.held_ref = bf16[8,8,4736]{2,1,0:T(8,128)(2,1)S(1)} all-to-all(bf16[8,8,4736]{2,1,0:T(8,128)(2,1)S(1)} %pack.1), channel_id=1, replica_groups={{0,2,4,6,7,5,3,1},{8,10,12,14,15,13,11,9},{16,18,20,22,23,21,19,17},{24..., dimensions={0} | all-to-all | bytes 1212416 | tf_op jit(solution)/shard_map/all_to_all | solution.py:476
  25.7 1.8 %select.9 = bf16[8,64,512]{2,1,0:T(8,128)(2,1)} custom-call(bf16[8,8,4736]{2,1,0:T(8,128)(2,1)S(1)} %all_to_all.15.held_ref), custom_call_target="tpu_custom_call" | custom-call | tf_op jit(solution)/shard_map/select/pallas_call | solution.py:480
  27.5 0.0 copy-start.1
  27.5 3.5 %all-to-all-start.1 = ((bf16[8,64,512]{2,1,0:T(8,128)(2,1)}), bf16[8,64,512]{2,1,0:T(8,128)(2,1)S(1)}, u32[]{:S(2)}, u32[]{:S(2)}) async-start(bf16[8,64,512]{2,1,0:T(8,128)(2,1)} %select.9), calls=%async_computation.1 | async-start | bytes 1048576 | tf_op jit(solution)/shard_map/all_to_all | solution.py:490
  31.0 0.0 copy-done.1
  33.0 0.0 copy-start
  33.0 0.2 convert_reduce_fusion.1
  33.2 0.5 copy-done
  33.7 0.2 convert_reduce_fusion
  33.9 0.6 multiply_add_fusion.1
  34.5 0.6 multiply_add_fusion
  35.0 1.4 %order.1 = (bf16[512,256]{1,0:T(8,128)(2,1)S(1)}, bf16[256,512]{1,0:T(8,128)(2,1)S(1)}, bf16[256,256]{1,0:T(8,128)(2,1)S(1)}, bf16[256,256]{1,0:T(8,128)(2,1)S(1...) custom-call(s32[1]{0:T(128)S(6)} %copy.16.counts_ref, s32[1,2]{1,0:T(1,128)} %hpattern_ref.1, f32[1]{0:T(128)S(6)} %copy.14.weight_ref, ...), custom_call_target="tpu_custom_call" | custom-call | tf_op jit(solution)/shard_map/order/pallas_call | solution.py:502
  36.5 7.1 %all-to-all-done.1 = bf16[8,64,512]{2,1,0:T(8,128)(2,1)S(1)} async-done(((bf16[8,64,512]{2,1,0:T(8,128)(2,1)}), bf16[8,64,512]{2,1,0:T(8,128)(2,1)S(1)}, u32[]{:S(2)}, u32[]{:S(2)}) %all-to-all-start.1) | async-done | bytes 524320 | tf_op jit(solution)/shard_map/all_to_all | solution.py:490
  43.6 1.1 %encode.1 = s16[32,56,128]{2,1,0:T(8,128)(2,1)S(1)} custom-call(bf16[512,512]{1,0:T(8,128)(2,1)S(1)} %bitcast.11, bf16[512,256]{1,0:T(8,128)(2,1)S(1)} %get-tuple-element.13.lower_ref, bf16[256,512]{1,0:T(8,128)(2,1)S(1)} %get-tuple-element.14.turned_ref, bf16[256,256]{1,0:T(8,128)(2,1)S(1)} %get-tuple-element.15.diag_ref, ...), custom_call_target="tpu_custom_call" | custom-call | tf_op jit(solution)/shard_map/encode/pallas_call | solution.py:531
  44.7 17.4 %all_to_all.16.recv_ref = s16[32,56,128]{2,1,0:T(8,128)(2,1)S(1)} all-to-all(s16[32,56,128]{2,1,0:T(8,128)(2,1)S(1)} %encode.1), channel_id=1, replica_groups={{0,16,24,8,2,18,26,10,4,20,28,12,6,22,30,14,7,23,31,15,5,21,29,13,3,19,..., dimensions={0} | all-to-all | bytes 917504 | tf_op jit(solution)/shard_map/all_to_all | solution.py:538
  62.1 1.2 %decode.1 = (bf16[192,256]{1,0:T(8,128)(2,1)}, bf16[192,256]{1,0:T(8,128)(2,1)}, f32[1,1]{1,0:T(1,128)}) custom-call(s32[8,256]{1,0:T(8,128)S(1)} %get-tuple-element.12.slots_ref, s16[32,56,128]{2,1,0:T(8,128)(2,1)S(1)} %all_to_all.16.recv_ref), custom_call_target="tpu_custom_call" | custom-call | tf_op jit(solution)/shard_map/decode/pallas_call | solution.py:547
  (2 shorter events, 0.0 us)
Async XLA Ops:
  27.5 3.5 %copy-start.1 = (s32[256]{0:T(256)S(1)}, s32[256]{0:T(256)}, u32[]{:S(2)}) copy-start(s32[256]{0:T(256)} %param.20) | copy-start | bytes 3076
  27.5 16.1 %all-to-all-start.1 = ((bf16[8,64,512]{2,1,0:T(8,128)(2,1)}), bf16[8,64,512]{2,1,0:T(8,128)(2,1)S(1)}, u32[]{:S(2)}, u32[]{:S(2)}) async-start(bf16[8,64,512]{2,1,0:T(8,128)(2,1)} %select.9), calls=%async_computation.1 | async-start | bytes 1048576 | tf_op jit(solution)/shard_map/all_to_all | solution.py:490
  33.0 0.7 %copy-start = (s32[256]{0:T(256)S(1)}, s32[256]{0:T(256)}, u32[]{:S(2)}) copy-start(s32[256]{0:T(256)} %param.21) | copy-start | bytes 3076

commit v10 on v9

--- a/solution.py
+++ b/solution.py
@@ -40,9 +40,11 @@
         )
         for c in range(stretches)
     ]
+    entries = pltpu.make_async_copy(table_hbm, table_ref, sems.at[stretches])
+    entries.start()
     for copy in copies:
         copy.start()
-    pltpu.sync_copy(table_hbm, table_ref)
+    entries.wait()
     lane = lax.broadcasted_iota(jnp.int32, (rows, LANES), 1)
     table = jnp.zeros((rows, LANES), jnp.float32)
     for m in range(table_ref.shape[1]):
@@ -469,7 +471,7 @@
             in_specs=[hspec(), hspec()],
             scratch_shapes=[
                 SMEM(ancestors.shape, jnp.int32),
-                pltpu.SemaphoreType.DMA((stretches,)),
+                pltpu.SemaphoreType.DMA((stretches + 1,)),
             ],
             name="pack",
         )(ancestors, anc_inv[0].reshape(stretches, grid_count, SUB, anc_rows))

time: 63.6 us -> 63.7 us (level)
  no operation moved by 1% of the time
where the time goes in v10:
time: 63.7 us; the launch traced here: 63.3 us
  blocking collectives  41.3 us (65%)
  waiting for transfers between devices  7.12 us (11%)
  Pallas kernels  6.67 us (10%)
  starting transfers between devices  3.5 us (5%)
  between operations  2.64 us (4%)
  other arithmetic  1.56 us (2%)
    all_to_all x1, blocking collectives, body(): lax.all_to_all(sent, 'grid', split_axis=0, concat_axis=0, axis_index_grou...  23.9 us
    all_to_all x1, blocking collectives, body(): lax.all_to_all(coded, ('pole', 'grid'), split_axis=0, concat_axis=0, axis...  17.4 us
    all_to_all x1, waiting for transfers between devices, body(): lax.all_to_all(chosen, 'grid', split_axis=0, concat_axis=0, axis_index_gr...  7.12 us
    all_to_all x1, starting transfers between devices, body(): lax.all_to_all(chosen, 'grid', split_axis=0, concat_axis=0, axis_index_gr...  3.5 us
    pallas_call x1, Pallas kernels, body(): pl.pallas_call(functools.partial(select_kernel, width, blk_count, stretch...  1.78 us
    pallas_call x1, Pallas kernels, body(): pl.pallas_call(order_kernel, out_shape=(VMEM((blk_count * width, width),...  1.43 us
  transfers between devices with their start and end apart: 1, of which 1 were waited for; matrix products, arithmetic and copies ran while one was open for 2% of the time, Pallas kernels for 2%

profile of v10, /device:TPU:0, one launch (start us, length us, event | category | flops | bytes accessed | tf_op | source)
XLA Modules:
  0.0 63.3 jit_solution(11302281359430224592)
XLA Ops:
  0.6 1.2 %pack.1 = bf16[8,8,4736]{2,1,0:T(8,128)(2,1)S(1)} custom-call(s32[1,2]{1,0:T(1,128)} %table_hbm.1, bf16[3,8,8,1536]{3,2,1,0:T(8,128)(2,1)} %bitcast.12), custom_call_target="tpu_custom_call" | custom-call | tf_op jit(solution)/shard_map/pack/pallas_call | solution.py:468
  1.8 23.9 %all_to_all.15.held_ref = bf16[8,8,4736]{2,1,0:T(8,128)(2,1)S(1)} all-to-all(bf16[8,8,4736]{2,1,0:T(8,128)(2,1)S(1)} %pack.1), channel_id=1, replica_groups={{0,2,4,6,7,5,3,1},{8,10,12,14,15,13,11,9},{16,18,20,22,23,21,19,17},{24..., dimensions={0} | all-to-all | bytes 1212416 | tf_op jit(solution)/shard_map/all_to_all | solution.py:478
  25.7 1.8 %select.9 = bf16[8,64,512]{2,1,0:T(8,128)(2,1)} custom-call(bf16[8,8,4736]{2,1,0:T(8,128)(2,1)S(1)} %all_to_all.15.held_ref), custom_call_target="tpu_custom_call" | custom-call | tf_op jit(solution)/shard_map/select/pallas_call | solution.py:482
  27.5 0.0 copy-start.1
  27.5 3.5 %all-to-all-start.1 = ((bf16[8,64,512]{2,1,0:T(8,128)(2,1)}), bf16[8,64,512]{2,1,0:T(8,128)(2,1)S(1)}, u32[]{:S(2)}, u32[]{:S(2)}) async-start(bf16[8,64,512]{2,1,0:T(8,128)(2,1)} %select.9), calls=%async_computation.1 | async-start | bytes 1048576 | tf_op jit(solution)/shard_map/all_to_all | solution.py:492
  31.0 0.0 copy-done.1
  33.0 0.0 copy-start
  33.0 0.2 convert_reduce_fusion.1
  33.2 0.5 copy-done
  33.7 0.2 convert_reduce_fusion
  33.9 0.6 multiply_add_fusion.1
  34.5 0.6 multiply_add_fusion
  35.1 1.4 %order.1 = (bf16[512,256]{1,0:T(8,128)(2,1)S(1)}, bf16[256,512]{1,0:T(8,128)(2,1)S(1)}, bf16[256,256]{1,0:T(8,128)(2,1)S(1)}, bf16[256,256]{1,0:T(8,128)(2,1)S(1...) custom-call(s32[1]{0:T(128)S(6)} %copy.16.counts_ref, s32[1,2]{1,0:T(1,128)} %hpattern_ref.1, f32[1]{0:T(128)S(6)} %copy.14.weight_ref, ...), custom_call_target="tpu_custom_call" | custom-call | tf_op jit(solution)/shard_map/order/pallas_call | solution.py:504
  36.5 7.1 %all-to-all-done.1 = bf16[8,64,512]{2,1,0:T(8,128)(2,1)S(1)} async-done(((bf16[8,64,512]{2,1,0:T(8,128)(2,1)}), bf16[8,64,512]{2,1,0:T(8,128)(2,1)S(1)}, u32[]{:S(2)}, u32[]{:S(2)}) %all-to-all-start.1) | async-done | bytes 524320 | tf_op jit(solution)/shard_map/all_to_all | solution.py:492
  43.6 1.1 %encode.1 = s16[32,56,128]{2,1,0:T(8,128)(2,1)S(1)} custom-call(bf16[512,512]{1,0:T(8,128)(2,1)S(1)} %bitcast.11, bf16[512,256]{1,0:T(8,128)(2,1)S(1)} %get-tuple-element.13.lower_ref, bf16[256,512]{1,0:T(8,128)(2,1)S(1)} %get-tuple-element.14.turned_ref, bf16[256,256]{1,0:T(8,128)(2,1)S(1)} %get-tuple-element.15.diag_ref, ...), custom_call_target="tpu_custom_call" | custom-call | tf_op jit(solution)/shard_map/encode/pallas_call | solution.py:533
  44.7 17.4 %all_to_all.16.recv_ref = s16[32,56,128]{2,1,0:T(8,128)(2,1)S(1)} all-to-all(s16[32,56,128]{2,1,0:T(8,128)(2,1)S(1)} %encode.1), channel_id=1, replica_groups={{0,16,24,8,2,18,26,10,4,20,28,12,6,22,30,14,7,23,31,15,5,21,29,13,3,19,..., dimensions={0} | all-to-all | bytes 917504 | tf_op jit(solution)/shard_map/all_to_all | solution.py:540
  62.1 1.2 %decode.1 = (bf16[192,256]{1,0:T(8,128)(2,1)}, bf16[192,256]{1,0:T(8,128)(2,1)}, f32[1,1]{1,0:T(1,128)}) custom-call(s32[8,256]{1,0:T(8,128)S(1)} %get-tuple-element.12.slots_ref, s16[32,56,128]{2,1,0:T(8,128)(2,1)S(1)} %all_to_all.16.recv_ref), custom_call_target="tpu_custom_call" | custom-call | tf_op jit(solution)/shard_map/decode/pallas_call | solution.py:549
  (2 shorter events, 0.0 us)
Async XLA Ops:
  27.5 3.5 %copy-start.1 = (s32[256]{0:T(256)S(1)}, s32[256]{0:T(256)}, u32[]{:S(2)}) copy-start(s32[256]{0:T(256)} %param.20) | copy-start | bytes 3076
  27.5 16.1 %all-to-all-start.1 = ((bf16[8,64,512]{2,1,0:T(8,128)(2,1)}), bf16[8,64,512]{2,1,0:T(8,128)(2,1)S(1)}, u32[]{:S(2)}, u32[]{:S(2)}) async-start(bf16[8,64,512]{2,1,0:T(8,128)(2,1)} %select.9), calls=%async_computation.1 | async-start | bytes 1048576 | tf_op jit(solution)/shard_map/all_to_all | solution.py:492
  33.0 0.7 %copy-start = (s32[256]{0:T(256)S(1)}, s32[256]{0:T(256)}, u32[]{:S(2)}) copy-start(s32[256]{0:T(256)} %param.21) | copy-start | bytes 3076
